TPU v7x, 1024 devices: a whole 8x8x8 slice. The times are simulated.
1024 devices in a mesh: gx: 16 (over x, core), gy: 64 (over y, z).
Axes of the slice: x: 8, y: 8, z: 8, core: 2. Of those that a mesh axis runs over, the one named last changes fastest.
Arguments:
- model_state: float32 [64, 2048, 528], P('gx', 'gy'), may hold values from -6 to 6
- hyper_coef: float32 [528], replicated, may hold values from 0.0001 to 0.001
- point_mass: float32 [64, 2048], P('gx', 'gy'), may hold values from 0.5 to 2
- inverse_mass: float32 [64, 2048], P('gx', 'gy'), may hold values from 0.2 to 0.8
- span_slot: int32 [64, 2048], P('gx', 'gy'), may hold values from 0 to 2047, as said below
- vert_diff: float32 [64, 48, 2048], P('gy', None, 'gx'), may hold values from 0.05 to 20
- fall_rate: float32 [64, 48, 2048], P('gy', None, 'gx'), may hold values from 0.1 to 10
- cloud_frac: float32 [64, 48, 2048], P('gy', None, 'gx'), may hold values from 0 to 1
Outputs:
- new_state: float32 [64, 2048, 528], P('gx', 'gy')
Inputs may be any that keep to these rules, and one draw needn't show every extreme that they name: `span_slot`: within the columns that share a block of 32 along the second dimension, the values form a permutation; each device's 128 columns hold exactly 8 values in each range from p * 128 to (p + 1) * 128 - 1.
All inputs are finite; a program needn't handle non-finite values.
Results may differ from a plain program's by a relative error of at most 0.0003.
Values sent between devices are 32-bit elements; how exact they have to be, the bound alone decides.
A program may use at most 32 MiB of HBM per device.

v0:
```python
import jax
import jax.numpy as jnp
import numpy as np
from jax import lax
from jax.sharding import PartitionSpec as P


def extended(block, sides, width):
    for axis, dim in sides:
        count = lax.axis_size(axis)
        forward = [(i, i + 1) for i in range(count - 1)]
        forward.append((count - 1, 0))
        backward = [(target, source) for source, target in forward]
        low = lax.ppermute(
            lax.slice_in_dim(block, block.shape[dim] - width, None, axis=dim), axis, forward
        )
        high = lax.ppermute(lax.slice_in_dim(block, 0, width, axis=dim), axis, backward)
        block = jnp.concatenate([low, block, high], axis=dim)
    return block


def second_table():
    nodes = np.array([-1.0, -1.0 / np.sqrt(5.0), 1.0 / np.sqrt(5.0), 1.0])
    deriv = np.zeros((4, 4))
    for row_index in range(4):
        for col_index in range(4):
            if row_index == col_index:
                deriv[row_index, col_index] = sum(
                    (
                        1.0 / (nodes[row_index] - nodes[other])
                        for other in range(4)
                        if other != row_index
                    )
                )
            else:
                upper_part = np.prod(
                    [nodes[row_index] - nodes[other] for other in range(4) if other != row_index]
                )
                lower_part = np.prod(
                    [nodes[col_index] - nodes[other] for other in range(4) if other != col_index]
                )
                deriv[row_index, col_index] = upper_part / (
                    lower_part * (nodes[row_index] - nodes[col_index])
                )
    return deriv @ deriv


def harmonic_operator(field):
    second_deriv = jnp.asarray(second_table(), jnp.float32)
    size_x, size_y, row_width = field.shape
    along_x = jnp.einsum(
        "ab,ebyf->eayf",
        second_deriv,
        field.reshape(size_x // 4, 4, size_y, row_width),
        precision=lax.Precision.HIGHEST,
    ).reshape(size_x, size_y, row_width)
    along_y = jnp.einsum(
        "ab,xebf->xeaf",
        second_deriv,
        field.reshape(size_x, size_y // 4, 4, row_width),
        precision=lax.Precision.HIGHEST,
    ).reshape(size_x, size_y, row_width)
    return along_x + along_y


def assemble(values, point_mass, inverse_mass):
    weighted = point_mass[:, :, None] * values
    size_x, size_y = point_mass.shape
    padded = extended(weighted, (("gx", 0), ("gy", 1)), 1)
    first_x = (jnp.arange(size_x) % 4 == 0)[:, None, None]
    last_x = (jnp.arange(size_x) % 4 == 3)[:, None, None]
    first_y = (jnp.arange(size_y) % 4 == 0)[None, :, None]
    last_y = (jnp.arange(size_y) % 4 == 3)[None, :, None]
    total = (
        weighted
        + jnp.where(first_x, padded[:-2, 1:-1], 0.0)
        + jnp.where(last_x, padded[2:, 1:-1], 0.0)
    )
    total = (
        total
        + jnp.where(first_y, padded[1:-1, :-2], 0.0)
        + jnp.where(last_y, padded[1:-1, 2:], 0.0)
    )
    total = total + jnp.where(first_x & first_y, padded[:-2, :-2], 0.0)
    total = total + jnp.where(first_x & last_y, padded[:-2, 2:], 0.0)
    total = total + jnp.where(last_x & first_y, padded[2:, :-2], 0.0)
    total = total + jnp.where(last_x & last_y, padded[2:, 2:], 0.0)
    return inverse_mass[:, :, None] * total


def physics(fields, diff_coef, fall_coef, overcast_fraction_weight):
    zero_row = jnp.zeros_like(diff_coef[:1])
    above = jnp.concatenate([zero_row, diff_coef[1:]], 0)
    below = jnp.concatenate([diff_coef[1:], zero_row], 0)
    surface = jnp.concatenate([jnp.zeros_like(diff_coef[1:]), diff_coef[:1]], 0)
    centre = 1.0 + above + below + surface

    def forward(state_carry, inputs):
        prev_gain, previous_value = state_carry
        sub_k, centre_k, sup_k, rhs_k = inputs
        divisor = centre_k - sub_k * prev_gain
        gain = sup_k / divisor
        value = (rhs_k + sub_k[None, :] * previous_value) / divisor[None, :]
        return ((gain, value), (gain, value))

    start = (jnp.zeros_like(diff_coef[0]), jnp.zeros_like(fields[0]))
    _, (gains, values) = lax.scan(forward, start, (above, centre, below, fields))

    def backward(next_solved, inputs):
        gain, value = inputs
        solved_line_entries = value + gain[None, :] * next_solved
        return (solved_line_entries, solved_line_entries)

    _, solved_line_entries = lax.scan(
        backward, jnp.zeros_like(fields[0]), (gains, values), reverse=True
    )
    thermal_state_kelvin = solved_line_entries[:, 0]
    humidity_mixing_ratio = solved_line_entries[:, 1]
    droplet_mixing_ratio = solved_line_entries[:, 2]
    condensed_mass_content = (
        overcast_fraction_weight
        * 0.5
        * jnp.maximum(humidity_mixing_ratio - 0.3 * thermal_state_kelvin, 0.0)
    )
    humidity_mixing_ratio = humidity_mixing_ratio - condensed_mass_content
    droplet_mixing_ratio = droplet_mixing_ratio + condensed_mass_content
    thermal_state_kelvin = thermal_state_kelvin + 2.0 * condensed_mass_content

    def settle(inflow, inputs):
        liquid_k, fall_k = inputs
        settled = (liquid_k + inflow) / (1.0 + fall_k)
        return (fall_k * settled, settled)

    _, droplet_mixing_ratio = lax.scan(
        settle, jnp.zeros_like(droplet_mixing_ratio[0]), (droplet_mixing_ratio, fall_coef)
    )
    return jnp.concatenate(
        [
            thermal_state_kelvin[:, None],
            humidity_mixing_ratio[:, None],
            droplet_mixing_ratio[:, None],
            solved_line_entries[:, 3:],
        ],
        1,
    )


def local(
    model_state, hyper_coef, point_mass, inverse_mass, span_slot, vert_diff, fall_rate, cloud_frac
):
    lap_once = assemble(harmonic_operator(model_state), point_mass, inverse_mass)
    lap_twice = assemble(harmonic_operator(lap_once), point_mass, inverse_mass)
    dynamic = model_state - hyper_coef[None, None, :] * lap_twice
    size_x, size_y, row_width = dynamic.shape
    levels = vert_diff.shape[1]
    variables = row_width // levels
    columns = size_x * size_y
    peers = lax.axis_size("gx")
    per_peer = columns // peers
    flat_state = dynamic.reshape(columns, row_width)
    position_labels = span_slot.reshape(columns)
    owner_order = jnp.argsort(position_labels // columns, stable=True)
    inverse_order = jnp.argsort(owner_order)
    sent_slots = position_labels[owner_order].reshape(peers, per_peer)
    local_diff = vert_diff[0]
    local_fall = fall_rate[0]
    local_cloud = cloud_frac[0]
    packed = flat_state[owner_order].reshape(peers, per_peer, row_width)
    arrived, arrived_slots = (
        lax.all_to_all(packed, "gx", split_axis=0, concat_axis=0, tiled=True),
        lax.all_to_all(sent_slots, "gx", split_axis=0, concat_axis=0, tiled=True),
    )
    local_slot = arrived_slots.reshape(columns) % columns
    fields = arrived.reshape(columns, variables, levels).transpose(2, 1, 0)
    updated = physics(
        fields,
        jnp.take(local_diff, local_slot, axis=1),
        jnp.take(local_fall, local_slot, axis=1),
        jnp.take(local_cloud, local_slot, axis=1),
    )
    tendency = (updated - fields).transpose(2, 1, 0).reshape(peers, per_peer, row_width)
    result_value = lax.all_to_all(tendency, "gx", split_axis=0, concat_axis=0, tiled=True)
    own_tendency = result_value.reshape(columns, row_width)[inverse_order]
    result = flat_state + own_tendency
    return result.reshape(size_x, size_y, row_width)


def solution(mesh):
    placed = (
        P("gx", "gy", None),
        P(),
        P("gx", "gy"),
        P("gx", "gy"),
        P("gx", "gy"),
        P("gy", None, "gx"),
        P("gy", None, "gx"),
        P("gy", None, "gx"),
    )
    return jax.shard_map(
        local, mesh=mesh, in_specs=placed, out_specs=P("gx", "gy", None), check_vma=False
    )
```

profile of v0, /device:TPU:1, one launch (start us, length us, event | category | flops | bytes accessed | tf_op | source)
XLA Modules:
  0.0 156.7 jit_solution(3763335738570369430)
XLA Ops:
  0.0 0.8 copy.93
  0.8 1.1 reshape.168
  2.8 0.7 copy-done
  3.5 0.8 fusion.12
  4.5 2.6 %collective-permute-start = (f32[1,32,528]{2,0,1:T(1,128)S(1)}, f32[1,32,528]{2,0,1:T(1,128)S(1)}, u32[]{:S(2)}, u32[]{:S(2)}) collective-permute-start(f32[1,32,528]{2,0,1:T(1,128)S(1)} %get-tuple-element.376), channel_id=1, source_target_pairs={{0,64},{64,128},{128,192},{192,256},{256,320},{320,384},{384,448},... | collective-permute-start | bytes 202760 | tf_op jit(solution)/shard_map/ppermute | solution.py:14
  7.1 11.6 %collective-permute-start.1 = (f32[1,32,528]{2,0,1:T(1,128)S(1)}, f32[1,32,528]{2,0,1:T(1,128)S(1)}, u32[]{:S(2)}, u32[]{:S(2)}) collective-permute-start(f32[1,32,528]{2,0,1:T(1,128)S(1)} %get-tuple-element.377), channel_id=1, source_target_pairs={{64,0},{128,64},{192,128},{256,192},{320,256},{384,320},{448,384},... | collective-permute-start | bytes 202760 | tf_op jit(solution)/shard_map/ppermute | solution.py:17
  18.9 2.5 %sort.34 = (s32[128]{0:T(128)}, s32[128]{0:T(128)S(1)}) sort(s32[128]{0:T(128)S(1)} %and_select_fusion.1, s32[128]{0:T(128)S(1)} %iota.66), dimensions={0}, to_apply=%region_0.1 | sort | flops 896 | bytes 2048 | tf_op jit(solution)/shard_map/jit(argsort)/sort | solution.py:162
  21.4 1.9 %collective-permute-start.2 = (f32[6,1,528]{2,0,1:T(8,128)S(1)}, f32[6,1,528]{2,0,1:T(8,128)S(1)}, u32[]{:S(2)}, u32[]{:S(2)}) collective-permute-start(f32[6,1,528]{2,0,1:T(8,128)S(1)} %get-tuple-element.372), channel_id=1, source_target_pairs={{0,1},{1,2},{2,3},{3,4},{4,5},{5,6},{6,7},{7,8},{8,9},{9,10},{10,1... | collective-permute-start | bytes 38024 | tf_op jit(solution)/shard_map/ppermute | solution.py:14
  23.4 10.3 %collective-permute-start.3 = (f32[6,1,528]{2,0,1:T(8,128)S(1)}, f32[6,1,528]{2,0,1:T(8,128)S(1)}, u32[]{:S(2)}, u32[]{:S(2)}) collective-permute-start(f32[6,1,528]{2,0,1:T(8,128)S(1)} %get-tuple-element.373), channel_id=1, source_target_pairs={{1,0},{2,1},{3,2},{4,3},{5,4},{6,5},{7,6},{8,7},{9,8},{10,9},{11,1... | collective-permute-start | bytes 38024 | tf_op jit(solution)/shard_map/ppermute | solution.py:17
  33.8 0.8 collective-permute-done.3
  34.8 1.0 fusion.28
  36.7 0.7 fusion.11
  37.6 1.5 collective-permute-start.4
  39.2 1.2 gather_fusion
  41.2 9.7 %all-to-all-start = ((s32[16,1,8]{2,1,0:T(1,128)}), s32[16,1,8]{2,1,0:T(1,128)S(1)}, u32[]{:S(2)}, u32[]{:S(2)}) async-start(s32[16,1,8]{2,1,0:T(1,128)} %bitcast.12), calls=%async_computation | async-start | bytes 16384 | tf_op jit(solution)/shard_map/all_to_all | solution.py:171
  52.5 5.4 %all-to-all-done = s32[16,1,8]{2,1,0:T(1,128)S(1)} async-done(((s32[16,1,8]{2,1,0:T(1,128)}), s32[16,1,8]{2,1,0:T(1,128)S(1)}, u32[]{:S(2)}, u32[]{:S(2)}) %all-to-all-start) | async-done | bytes 544 | tf_op jit(solution)/shard_map/all_to_all | solution.py:171
  59.2 1.9 %collective-permute-start.6 = (f32[6,1,528]{2,0,1:T(8,128)S(1)}, f32[6,1,528]{2,0,1:T(8,128)S(1)}, u32[]{:S(2)}, u32[]{:S(2)}) collective-permute-start(f32[6,1,528]{2,0,1:T(8,128)S(1)} %get-tuple-element.368), channel_id=1, source_target_pairs={{0,1},{1,2},{2,3},{3,4},{4,5},{5,6},{6,7},{7,8},{8,9},{9,10},{10,1... | collective-permute-start | bytes 38024 | tf_op jit(solution)/shard_map/ppermute | solution.py:14
  61.1 7.2 %collective-permute-start.7 = (f32[6,1,528]{2,0,1:T(8,128)S(1)}, f32[6,1,528]{2,0,1:T(8,128)S(1)}, u32[]{:S(2)}, u32[]{:S(2)}) collective-permute-start(f32[6,1,528]{2,0,1:T(8,128)S(1)} %get-tuple-element.369), channel_id=1, source_target_pairs={{1,0},{2,1},{3,2},{4,3},{5,4},{6,5},{7,6},{8,7},{9,8},{10,9},{11,1... | collective-permute-start | bytes 38024 | tf_op jit(solution)/shard_map/ppermute | solution.py:17
  68.4 0.9 collective-permute-done.7
  69.9 1.2 fusion.17
  71.1 1.5 gather_fusion.1
  72.7 4.8 %all-to-all-start.1 = ((f32[16,8,528]{2,1,0:T(8,128)}), f32[16,8,528]{2,1,0:T(8,128)S(1)}, u32[]{:S(2)}, u32[]{:S(2)}) async-start(f32[16,8,528]{2,1,0:T(8,128)} %bitcast.16), calls=%async_computation.1 | async-start | bytes 655360 | tf_op jit(solution)/shard_map/all_to_all | solution.py:170
  79.3 1.3 gather_fusion.4
  81.2 9.6 %all-to-all-done.1 = f32[16,8,528]{2,1,0:T(8,128)S(1)} async-done(((f32[16,8,528]{2,1,0:T(8,128)}), f32[16,8,528]{2,1,0:T(8,128)S(1)}, u32[]{:S(2)}, u32[]{:S(2)}) %all-to-all-start.1) | async-done | bytes 270368 | tf_op jit(solution)/shard_map/all_to_all | solution.py:170
  91.8 5.6 %while.47 = (s32[]{:T(128)}, f32[128]{0:T(128)S(1)}, f32[11,128]{1,0:T(8,128)S(1)}, f32[48,128]{1,0:T(8,128)S(1)}, f32[48,11,128]{2,1,0:T(8,128)S(1)}, /*index=5...) while((s32[]{:T(128)}, f32[128]{0:T(128)S(1)}, ...), condition=%wide.region_2.4_spmd.clone, body=%wide.region_1.3_spmd.clone.sunk | while | flops 6147 | bytes 39048 | solution.py:107
  97.5 2.7 %while.48 = (s32[]{:T(128)}, f32[11,128]{1,0:T(8,128)S(1)}, f32[48,11,128]{2,1,0:T(8,128)S(1)}, f32[48,11,128]{2,1,0:T(8,128)S(1)}, f32[48,128]{1,0:T(8,128)S(1)}, /*index=5*/s32[]{:T(128)}, s32[]{:T(128)}, s32[]{:T(128)}) while((s32[]{:T(128)}, f32[11,128]{1,0:T(8,128)S(1)}, f32[48,11,128]{2,1,0:T(8,128)S(1)}, ...), condition=%wide.region_4.6_spmd.clone, body=%wide.region_3.5_spmd.clone.sunk | while | flops 4228 | bytes 34419 | solution.py:114
  101.0 0.9 multiply_add_fusion
  102.0 35.4 %while.49 = (s32[]{:T(128)}, f32[128]{0:T(128)S(1)}, f32[48,128]{1,0:T(8,128)S(1)}, f32[48,128]{1,0:T(8,128)}, f32[48,128]{1,0:T(8,128)S(1)}, /*index=5*/s32[]{:T(128)}, s32[]{:T(128)}) while((s32[]{:T(128)}, f32[128]{0:T(128)S(1)}, f32[48,128]{1,0:T(8,128)S(1)}, f32[48,128]{1,0:T(8,128)}, f32[48,128]{1,0:T(8,128)S(1)}, ...), condition=%wide.region_6.8_spmd.clone, body=%wide.region_5.7_spmd.clone.sunk | while | flops 643 | bytes 3679 | solution.py:134
  102.1 0.7 bitcast_multiply_fusion.3
  102.8 0.7 bitcast_multiply_fusion.3
  103.6 0.7 bitcast_multiply_fusion.3
  104.3 0.7 bitcast_multiply_fusion.3
  105.0 0.7 bitcast_multiply_fusion.3
  105.8 0.7 bitcast_multiply_fusion.3
  106.5 0.7 bitcast_multiply_fusion.3
  107.3 0.7 bitcast_multiply_fusion.3
  113.8 0.7 bitcast_multiply_fusion.3
  114.6 0.7 bitcast_multiply_fusion.3
  115.3 0.7 bitcast_multiply_fusion.3
  116.1 0.7 bitcast_multiply_fusion.3
  116.8 0.7 bitcast_multiply_fusion.3
  119.0 0.7 bitcast_multiply_fusion.3
  138.1 1.0 reshape.178
  139.1 3.4 %all-to-all-start.2 = ((f32[16,8,528]{2,1,0:T(8,128)}), f32[16,8,528]{2,1,0:T(8,128)S(1)}, u32[]{:S(2)}, u32[]{:S(2)}) async-start(f32[16,8,528]{2,1,0:T(8,128)} %reshape.178), calls=%async_computation.2 | async-start | bytes 655360 | tf_op jit(solution)/shard_map/all_to_all | solution.py:182
  142.6 2.6 %sort.35 = (s32[128]{0:T(128)}, s32[128]{0:T(128)S(1)}) sort(s32[128]{0:T(128)S(1)} %get-tuple-element.186, s32[128]{0:T(128)S(1)} %iota.67), dimensions={0}, to_apply=%region_7.9 | sort | flops 896 | bytes 2048 | tf_op jit(solution)/shard_map/jit(argsort)/sort | solution.py:163
  145.2 9.6 %all-to-all-done.2 = f32[16,8,528]{2,1,0:T(8,128)S(1)} async-done(((f32[16,8,528]{2,1,0:T(8,128)}), f32[16,8,528]{2,1,0:T(8,128)S(1)}, u32[]{:S(2)}, u32[]{:S(2)}) %all-to-all-start.2) | async-done | bytes 270368 | tf_op jit(solution)/shard_map/all_to_all | solution.py:182
  154.8 0.8 gather_fusion.2
  155.9 0.7 copy.120
  (453 shorter events, 42.1 us)
Async XLA Ops:
  0.8 1.1 copy-start.4
  2.5 1.0 copy-start
  2.5 1.0 copy-start.5
  4.5 16.9 %collective-permute-start = (f32[1,32,528]{2,0,1:T(1,128)S(1)}, f32[1,32,528]{2,0,1:T(1,128)S(1)}, u32[]{:S(2)}, u32[]{:S(2)}) collective-permute-start(f32[1,32,528]{2,0,1:T(1,128)S(1)} %get-tuple-element.376), channel_id=1, source_target_pairs={{0,64},{64,128},{128,192},{192,256},{256,320},{320,384},{384,448},... | collective-permute-start | bytes 202760 | tf_op jit(solution)/shard_map/ppermute | solution.py:14
  7.1 11.6 %copy-start.8 = (s32[4,32]{1,0:T(4,128)S(1)}, s32[4,32]{1,0:T(4,128)}, u32[]{:S(2)}) copy-start(s32[4,32]{1,0:T(4,128)} %param.22) | copy-start | bytes 1540
  7.1 14.3 %collective-permute-start.1 = (f32[1,32,528]{2,0,1:T(1,128)S(1)}, f32[1,32,528]{2,0,1:T(1,128)S(1)}, u32[]{:S(2)}, u32[]{:S(2)}) collective-permute-start(f32[1,32,528]{2,0,1:T(1,128)S(1)} %get-tuple-element.377), channel_id=1, source_target_pairs={{64,0},{128,64},{192,128},{256,192},{320,256},{384,320},{448,384},... | collective-permute-start | bytes 202760 | tf_op jit(solution)/shard_map/ppermute | solution.py:17
  21.4 12.3 %collective-permute-start.2 = (f32[6,1,528]{2,0,1:T(8,128)S(1)}, f32[6,1,528]{2,0,1:T(8,128)S(1)}, u32[]{:S(2)}, u32[]{:S(2)}) collective-permute-start(f32[6,1,528]{2,0,1:T(8,128)S(1)} %get-tuple-element.372), channel_id=1, source_target_pairs={{0,1},{1,2},{2,3},{3,4},{4,5},{5,6},{6,7},{7,8},{8,9},{9,10},{10,1... | collective-permute-start | bytes 38024 | tf_op jit(solution)/shard_map/ppermute | solution.py:14
  23.4 10.3 %copy-start.7 = (f32[4,32]{1,0:T(4,128)S(1)}, f32[4,32]{1,0:T(4,128)}, u32[]{:S(2)}) copy-start(f32[4,32]{1,0:T(4,128)} %param.21) | copy-start | bytes 1540
  23.4 11.2 %collective-permute-start.3 = (f32[6,1,528]{2,0,1:T(8,128)S(1)}, f32[6,1,528]{2,0,1:T(8,128)S(1)}, u32[]{:S(2)}, u32[]{:S(2)}) collective-permute-start(f32[6,1,528]{2,0,1:T(8,128)S(1)} %get-tuple-element.373), channel_id=1, source_target_pairs={{1,0},{2,1},{3,2},{4,3},{5,4},{6,5},{7,6},{8,7},{9,8},{10,9},{11,1... | collective-permute-start | bytes 38024 | tf_op jit(solution)/shard_map/ppermute | solution.py:17
  37.6 21.5 %collective-permute-start.4 = (f32[1,32,528]{2,0,1:T(1,128)S(1)}, f32[1,32,528]{2,0,1:T(1,128)S(1)}, u32[]{:S(2)}, u32[]{:S(2)}) collective-permute-start(f32[1,32,528]{2,0,1:T(1,128)S(1)} %get-tuple-element.374), channel_id=1, source_target_pairs={{0,64},{64,128},{128,192},{192,256},{256,320},{320,384},{384,448},... | collective-permute-start | bytes 202760 | tf_op jit(solution)/shard_map/ppermute | solution.py:14
  39.1 20.0 %collective-permute-start.5 = (f32[1,32,528]{2,0,1:T(1,128)S(1)}, f32[1,32,528]{2,0,1:T(1,128)S(1)}, u32[]{:S(2)}, u32[]{:S(2)}) collective-permute-start(f32[1,32,528]{2,0,1:T(1,128)S(1)} %get-tuple-element.375), channel_id=1, source_target_pairs={{64,0},{128,64},{192,128},{256,192},{320,256},{384,320},{448,384},... | collective-permute-start | bytes 202760 | tf_op jit(solution)/shard_map/ppermute | solution.py:17
  40.5 10.4 %copy-start.1 = (f32[1,48,128]{2,1,0:T(8,128)S(1)}, f32[1,48,128]{2,1,0:T(8,128)}, u32[]{:S(2)}) copy-start(f32[1,48,128]{2,1,0:T(8,128)} %param.23) | copy-start | bytes 73732
  41.2 16.7 %all-to-all-start = ((s32[16,1,8]{2,1,0:T(1,128)}), s32[16,1,8]{2,1,0:T(1,128)S(1)}, u32[]{:S(2)}, u32[]{:S(2)}) async-start(s32[16,1,8]{2,1,0:T(1,128)} %bitcast.12), calls=%async_computation | async-start | bytes 16384 | tf_op jit(solution)/shard_map/all_to_all | solution.py:171
  50.9 0.7 copy-start.2
  51.7 0.7 copy-start.3
  59.2 9.2 %collective-permute-start.6 = (f32[6,1,528]{2,0,1:T(8,128)S(1)}, f32[6,1,528]{2,0,1:T(8,128)S(1)}, u32[]{:S(2)}, u32[]{:S(2)}) collective-permute-start(f32[6,1,528]{2,0,1:T(8,128)S(1)} %get-tuple-element.368), channel_id=1, source_target_pairs={{0,1},{1,2},{2,3},{3,4},{4,5},{5,6},{6,7},{7,8},{8,9},{9,10},{10,1... | collective-permute-start | bytes 38024 | tf_op jit(solution)/shard_map/ppermute | solution.py:14
  61.1 8.1 %collective-permute-start.7 = (f32[6,1,528]{2,0,1:T(8,128)S(1)}, f32[6,1,528]{2,0,1:T(8,128)S(1)}, u32[]{:S(2)}, u32[]{:S(2)}) collective-permute-start(f32[6,1,528]{2,0,1:T(8,128)S(1)} %get-tuple-element.369), channel_id=1, source_target_pairs={{1,0},{2,1},{3,2},{4,3},{5,4},{6,5},{7,6},{8,7},{9,8},{10,9},{11,1... | collective-permute-start | bytes 38024 | tf_op jit(solution)/shard_map/ppermute | solution.py:17
  69.2 0.7 copy-start.6
  72.7 18.1 %all-to-all-start.1 = ((f32[16,8,528]{2,1,0:T(8,128)}), f32[16,8,528]{2,1,0:T(8,128)S(1)}, u32[]{:S(2)}, u32[]{:S(2)}) async-start(f32[16,8,528]{2,1,0:T(8,128)} %bitcast.16), calls=%async_computation.1 | async-start | bytes 655360 | tf_op jit(solution)/shard_map/all_to_all | solution.py:170
  139.1 15.7 %all-to-all-start.2 = ((f32[16,8,528]{2,1,0:T(8,128)}), f32[16,8,528]{2,1,0:T(8,128)S(1)}, u32[]{:S(2)}, u32[]{:S(2)}) async-start(f32[16,8,528]{2,1,0:T(8,128)} %reshape.178), calls=%async_computation.2 | async-start | bytes 655360 | tf_op jit(solution)/shard_map/all_to_all | solution.py:182
where the time goes:
time: 159 us; the launch traced here: 157 us
  starting transfers between devices  55.2 us (35%)
  other arithmetic  46.1 us (29%)
  waiting for transfers between devices  26.2 us (16%)
  local copies, waits for them, and re-layouts  21.8 us (14%)
  loops' own time  4.04 us (3%)
  matrix products  2.9 us (2%)
    mul x48, other arithmetic, settle(): return (fall_k * settled, settled)  33.3 us
    ppermute x4, starting transfers between devices, extended(): lax.ppermute(lax.slice_in_dim(block, 0, width, axis=dim), axis, backward)  29.2 us
    all_to_all x1, starting transfers between devices, local(): lax.all_to_all(sent_slots, 'gx', split_axis=0, concat_axis=0, tiled=True)  9.7 us
    all_to_all x1, waiting for transfers between devices, local(): lax.all_to_all(tendency, 'gx', split_axis=0, concat_axis=0, tiled=True)  9.62 us
    all_to_all x1, waiting for transfers between devices, local(): lax.all_to_all(packed, 'gx', split_axis=0, concat_axis=0, tiled=True)  9.6 us
    ppermute x4, starting transfers between devices, extended(): lax.ppermute(lax.slice_in_dim(block, block.shape[dim] - width, None, axis...  7.98 us
    all_to_all x1, waiting for transfers between devices, local(): lax.all_to_all(sent_slots, 'gx', split_axis=0, concat_axis=0, tiled=True)  5.36 us
    unnamed x28, local copies, waits for them, and re-layouts  5 us
  transfers between devices with their start and end apart: 11, of which 5 were waited for; matrix products, arithmetic and copies ran while one was open for 8% of the time, Pallas kernels for 0%

commit v1 on v0

v1 whole, which is shorter than its diff:
```python
import functools

import jax
import jax.numpy as jnp
import numpy as np
from jax import lax
from jax.experimental import pallas as pl
from jax.experimental.pallas import tpu as pltpu
from jax.sharding import PartitionSpec as P

MESH = pl.DeviceIdType.MESH
F32 = jnp.float32
BF16 = jnp.bfloat16
NX, NY, COLS, LEV, VARS = 4, 32, 128, 48, 11
FLD = LEV * VARS
COEF = 3 * LEV


def second_table():
    nodes = np.array([-1.0, -1.0 / np.sqrt(5.0), 1.0 / np.sqrt(5.0), 1.0])
    deriv = np.zeros((4, 4))
    for i in range(4):
        for j in range(4):
            if i == j:
                deriv[i, j] = sum(1.0 / (nodes[i] - nodes[o]) for o in range(4) if o != i)
            else:
                upper = np.prod([nodes[i] - nodes[o] for o in range(4) if o != i])
                lower = np.prod([nodes[j] - nodes[o] for o in range(4) if o != j])
                deriv[i, j] = upper / (lower * (nodes[i] - nodes[j]))
    return (deriv @ deriv).astype(np.float32)


def tables():
    second = second_table()
    x, y = np.divmod(np.arange(COLS), NY)
    same_x = x[:, None] == x[None, :]
    same_y = y[:, None] == y[None, :]
    same_e = (y[:, None] // 4) == (y[None, :] // 4)
    lap = np.where(same_y, second[x[:, None], x[None, :]], 0.0)
    lap = lap + np.where(same_x & same_e, second[y[:, None] % 4, y[None, :] % 4], 0.0)
    twin = np.where(y % 4 == 0, y - 1, np.where(y % 4 == 3, y + 1, -5))
    pick = np.eye(COLS) + np.where(same_x & (y[None, :] == twin[:, None]), 1.0, 0.0)
    edge = np.zeros((8, COLS))
    for i in range(4):
        edge[i, i * NY] = 1.0
        edge[4 + i, i * NY + NY - 1] = 1.0
    return lap.astype(np.float32), np.concatenate([pick, edge], 0).astype(np.float32)


def split(value):
    high = value.astype(BF16)
    return high, (value - high.astype(F32)).astype(BF16)


def dot(a, b):
    return jnp.dot(a, b, preferred_element_type=F32)


def exact(a, b, dims):
    return lax.dot_general(
        a, b, (dims, ((), ())), precision=lax.Precision.HIGHEST, preferred_element_type=F32
    )


def iota(shape, dim):
    return lax.broadcasted_iota(jnp.int32, shape, dim)


def body(
    n_gx, n_gy,
    state, hyper, pmass, imass, slots, vdiff, frate, cfrac, lap, pick,
    out,
    v, tsum, edges, xin, yin, cin, small, sl, coef, sent, got, lap_s, pick_s, hyp,
    dyn, tr, fac, wk, res,
    in_sem, out_sem, hs_sem, hr_sem, ss_sem, sr_sem, cs_sem, cr_sem,
):
    per = COLS // n_gx
    me = lax.axis_index("gx")
    my = lax.axis_index("gy")
    left, right = lax.rem(me + n_gx - 1, n_gx), lax.rem(me + 1, n_gx)
    down, up = lax.rem(my + n_gy - 1, n_gy), lax.rem(my + 1, n_gy)
    peers = [lax.rem(me + i, n_gx) for i in range(1, n_gx)]
    around = [(left, my), (right, my), (me, down), (me, up),
              (left, down), (left, up), (right, down), (right, up)]

    barrier = pltpu.get_barrier_semaphore()
    for target in around[2:] + [(q, my) for q in peers]:
        pl.semaphore_signal(barrier, inc=1, device_id=target, device_id_type=MESH)

    loads = [
        pltpu.make_async_copy(slots, sl.at[me], in_sem.at[0]),
        pltpu.make_async_copy(pmass, small.at[0], in_sem.at[1]),
        pltpu.make_async_copy(imass, small.at[1], in_sem.at[2]),
        pltpu.make_async_copy(lap, lap_s, in_sem.at[3]),
        pltpu.make_async_copy(pick, pick_s, in_sem.at[4]),
        pltpu.make_async_copy(vdiff.at[0], coef.at[pl.ds(0, LEV)], in_sem.at[5]),
        pltpu.make_async_copy(frate.at[0], coef.at[pl.ds(LEV, LEV)], in_sem.at[6]),
        pltpu.make_async_copy(cfrac.at[0], coef.at[pl.ds(2 * LEV, LEV)], in_sem.at[7]),
        pltpu.make_async_copy(hyper, hyp, in_sem.at[8]),
    ] + [
        pltpu.make_async_copy(state.at[x], v.at[pl.ds(NY * x, NY)], in_sem.at[9 + x])
        for x in range(NX)
    ]
    for load in loads:
        load.start()

    rows, lanes = iota((COLS, COLS), 0), iota((COLS, COLS), 1)
    eye = rows == lanes
    tri = jnp.where(rows < lanes, 1.0, 0.0).astype(BF16)

    def as_row(block):
        return jnp.concatenate([block[x : x + 1, :] for x in range(NX)], axis=1)

    for i in (1, 2, 3, 4):
        loads[i].wait()
    mass_row = as_row(small[0])
    inv_row = as_row(small[1])
    inv_col = jnp.sum(jnp.where(eye, inv_row, 0.0), axis=1, keepdims=True)
    op_high, op_low = split(exact(pick_s[...] * mass_row, lap_s[...], ((1,), (0,))))

    def weigh(r, field):
        high, low = split(field)
        total = dot(op_high, high) + (dot(op_high, low) + dot(op_low, high))
        tsum[r] = total[:COLS]
        for i in range(8):
            edges[r, i] = total[COLS + i : COLS + i + 1]

    def halo(r):
        plan = [
            (tsum.at[r, pl.ds(0, NY)], xin.at[r, 1]),
            (tsum.at[r, pl.ds(COLS - NY, NY)], xin.at[r, 0]),
            (edges.at[r, pl.ds(0, 4)], yin.at[r, 1]),
            (edges.at[r, pl.ds(4, 4)], yin.at[r, 0]),
            (edges.at[r, 0], cin.at[r, 3]),
            (edges.at[r, 4], cin.at[r, 2]),
            (edges.at[r, 3], cin.at[r, 1]),
            (edges.at[r, 7], cin.at[r, 0]),
        ]
        return [
            pltpu.make_async_remote_copy(
                src_ref=src, dst_ref=dst, send_sem=hs_sem.at[r, i], recv_sem=hr_sem.at[r, i],
                device_id=around[i], device_id_type=MESH,
            )
            for i, (src, dst) in enumerate(plan)
        ]

    def assemble(r):
        acc = tsum.at[r]
        acc[pl.ds(0, NY), :] = acc[pl.ds(0, NY), :] + xin[r, 0]
        acc[pl.ds(COLS - NY, NY), :] = acc[pl.ds(COLS - NY, NY), :] + xin[r, 1]
        corner = {0: (0, 1), 3: (2, 3)}
        for x in range(NX):
            low, high = yin[r, 0, x], yin[r, 1, x]
            if x in corner:
                low = low + cin[r, corner[x][0]]
                high = high + cin[r, corner[x][1]]
            acc[pl.ds(NY * x, 1), :] = acc[pl.ds(NY * x, 1), :] + low
            acc[pl.ds(NY * x + NY - 1, 1), :] = acc[pl.ds(NY * x + NY - 1, 1), :] + high
        return inv_col * acc[...]

    for x in range(NX):
        loads[9 + x].wait()
    weigh(0, v[...])
    loads[0].wait()

    pl.semaphore_wait(barrier, n_gx - 1 + 6)

    slot_sends = [
        pltpu.make_async_remote_copy(
            src_ref=sl.at[me], dst_ref=sl.at[me], send_sem=ss_sem.at[i], recv_sem=sr_sem.at[me],
            device_id=(q, my), device_id_type=MESH,
        )
        for i, q in enumerate(peers)
    ]
    for copy in slot_sends:
        copy.start()
    first = halo(0)
    for copy in first:
        copy.start()

    own = as_row(sl[me])
    span = own // COLS
    member = jnp.where(span == iota((n_gx, COLS), 0), 1.0, 0.0)
    before = dot(member.astype(BF16), tri)
    rank = jnp.sum(member * before, axis=0, keepdims=True)
    place = span * per + rank.astype(jnp.int32)
    order = jnp.where(rows == place, 1.0, 0.0)

    for i in (5, 6, 7):
        loads[i].wait()
    for q in peers:
        pltpu.make_async_remote_copy(
            src_ref=sl.at[q], dst_ref=sl.at[q], send_sem=ss_sem.at[0], recv_sem=sr_sem.at[q],
            device_id=(q, my), device_id_type=MESH,
        ).wait_recv()
    every = jnp.concatenate([sl[:, x, :] for x in range(NX)], axis=1)
    mine = (every // COLS) == me
    member = jnp.where(mine, 1.0, 0.0)
    before = dot(member.astype(BF16), tri)
    ranked = jnp.where(mine, before, -1.0).astype(BF16)
    within = (every % COLS).astype(F32).astype(BF16)
    spread = jnp.where(
        iota((COLS, n_gx), 0) // per == iota((COLS, n_gx), 1), 1.0, 0.0
    ).astype(BF16)
    hit = dot(spread, ranked) == (rows % per).astype(F32)
    chosen = jnp.sum(jnp.where(hit, dot(spread, within), 0.0), axis=1, keepdims=True)
    onehot = jnp.where(chosen == lanes.astype(F32), 1.0, 0.0)
    picked = exact(onehot, coef[...], ((1,), (1,)))
    sent[...] = picked.reshape(n_gx, per, COEF)
    coef_sends = [
        pltpu.make_async_remote_copy(
            src_ref=sent.at[q], dst_ref=got.at[me], send_sem=cs_sem.at[i], recv_sem=cr_sem.at[me],
            device_id=(q, my), device_id_type=MESH,
        )
        for i, q in enumerate(peers)
    ]
    for copy in coef_sends:
        copy.start()
    got[me] = sent[me]

    for copy in first:
        copy.wait_recv()
    first[0].wait_send()
    first[1].wait_send()
    weigh(1, assemble(0))
    second = halo(1)
    for copy in second:
        copy.start()

    for q in peers:
        pltpu.make_async_remote_copy(
            src_ref=sent.at[q], dst_ref=got.at[q], send_sem=cs_sem.at[0], recv_sem=cr_sem.at[q],
            device_id=(q, my), device_id_type=MESH,
        ).wait_recv()
    mat = exact(got[...].reshape(COLS, COEF), order, ((0,), (0,)))
    diff, fall, cloud = mat[:LEV], mat[LEV : 2 * LEV], mat[2 * LEV :]
    level = iota((LEV, COLS), 0)
    above = jnp.where(level == 0, 0.0, diff)
    below = jnp.where(level == LEV - 1, 0.0, pltpu.roll(diff, LEV - 1, 0))
    surface = jnp.where(level == LEV - 1, diff[0:1], 0.0)
    centre = 1.0 + above + below + surface
    fac[0] = above
    fac[1] = below
    fac[2] = centre
    gain = jnp.zeros((1, COLS), F32)
    for k in range(LEV):
        a, b, c = (fac[j, pl.ds(k, 1), :] for j in range(3))
        scale = 1.0 / (c - a * gain)
        gain = b * scale
        fac[0, pl.ds(k, 1), :] = a * scale
        fac[1, pl.ds(k, 1), :] = gain
        fac[2, pl.ds(k, 1), :] = scale
    settle = 1.0 / (1.0 + fall)
    inflow = jnp.where(level == 0, 0.0, pltpu.roll(fall, 1, 0)) * settle
    fac[3] = settle
    fac[4] = inflow
    fac[5] = cloud * 0.5

    loads[8].wait()
    for copy in second:
        copy.wait_recv()
    second[0].wait_send()
    second[1].wait_send()
    dyn[:, pl.ds(0, FLD)] = v[...] - hyp[...] * assemble(1)
    for j in range(5):
        tr[pl.ds(COLS * j, COLS), :] = dyn[:, pl.ds(COLS * j, COLS)].T

    def strided(k):
        return pl.ds(k, VARS, stride=LEV)

    value = jnp.zeros((VARS, COLS), F32)
    for k in range(LEV):
        value = tr[strided(k), :] * fac[2, pl.ds(k, 1), :] + fac[0, pl.ds(k, 1), :] * value
        wk[k] = value
    value = jnp.zeros((VARS, COLS), F32)
    for k in reversed(range(LEV)):
        value = wk[k] + fac[1, pl.ds(k, 1), :] * value
        tr[strided(k), :] = value

    heat, vapour, liquid = (tr[pl.ds(LEV * j, LEV), :] for j in range(3))
    moved = fac[5] * jnp.maximum(vapour - 0.3 * heat, 0.0)
    tr[pl.ds(0, LEV), :] = heat + 2.0 * moved
    tr[pl.ds(LEV, LEV), :] = vapour - moved
    fac[3] = (liquid + moved) * fac[3]
    drop = jnp.zeros((1, COLS), F32)
    for k in range(LEV):
        drop = fac[3, pl.ds(k, 1), :] + fac[4, pl.ds(k, 1), :] * drop
        tr[pl.ds(2 * LEV + k, 1), :] = drop

    for j in range(5):
        width = min(COLS, FLD - COLS * j)
        res[:, pl.ds(COLS * j, width)] = tr[pl.ds(COLS * j, COLS), :].T[:, :width]
    stores = [
        pltpu.make_async_copy(res.at[pl.ds(NY * x, NY)], out.at[x], out_sem.at[x])
        for x in range(NX)
    ]
    for store in stores:
        store.start()
    for copy in slot_sends + coef_sends + first[2:] + second[2:]:
        copy.wait_send()
    for store in stores:
        store.wait()


def solution(mesh):
    n_gx, n_gy = mesh.shape["gx"], mesh.shape["gy"]
    per = COLS // n_gx
    lap, pick = tables()
    anywhere = pl.BlockSpec(memory_space=pl.ANY)
    dma = pltpu.SemaphoreType.DMA

    def local(state, hyper, pmass, imass, slots, vdiff, frate, cfrac):
        return pl.pallas_call(
            functools.partial(body, n_gx, n_gy),
            out_shape=jax.ShapeDtypeStruct((NX, NY, FLD), F32),
            in_specs=[anywhere] * 10,
            out_specs=anywhere,
            scratch_shapes=[
                pltpu.VMEM((COLS, FLD), F32),
                pltpu.VMEM((2, COLS, FLD), F32),
                pltpu.VMEM((2, 8, 1, FLD), F32),
                pltpu.VMEM((2, 2, NY, FLD), F32),
                pltpu.VMEM((2, 2, 4, 1, FLD), F32),
                pltpu.VMEM((2, 4, 1, FLD), F32),
                pltpu.VMEM((2, NX, NY), F32),
                pltpu.VMEM((n_gx, NX, NY), jnp.int32),
                pltpu.VMEM((COEF, COLS), F32),
                pltpu.VMEM((n_gx, per, COEF), F32),
                pltpu.VMEM((n_gx, per, COEF), F32),
                pltpu.VMEM((COLS, COLS), F32),
                pltpu.VMEM((COLS + 8, COLS), F32),
                pltpu.VMEM((1, FLD), F32),
                pltpu.VMEM((COLS, 5 * COLS), F32),
                pltpu.VMEM((5 * COLS, COLS), F32),
                pltpu.VMEM((6, LEV, COLS), F32),
                pltpu.VMEM((LEV, VARS, COLS), F32),
                pltpu.VMEM((COLS, FLD), F32),
                dma((13,)),
                dma((NX,)),
                dma((2, 8)),
                dma((2, 8)),
                dma((n_gx,)),
                dma((n_gx,)),
                dma((n_gx,)),
                dma((n_gx,)),
            ],
            compiler_params=pltpu.CompilerParams(collective_id=0, has_side_effects=True),
        )(state, hyper.reshape(1, FLD), pmass, imass, slots, vdiff, frate, cfrac,
          jnp.asarray(lap), jnp.asarray(pick))

    placed = (
        P("gx", "gy", None), P(), P("gx", "gy"), P("gx", "gy"), P("gx", "gy"),
        P("gy", None, "gx"), P("gy", None, "gx"), P("gy", None, "gx"),
    )
    return jax.shard_map(
        local, mesh=mesh, in_specs=placed, out_specs=P("gx", "gy", None), check_vma=False
    )
```

time: 159 us -> 41.5 us (0.26); the launches traced: 157 us -> 41.3 us
  starting transfers between devices: 55.2 us -> 0 us
  other arithmetic: 46.1 us -> 0 us
  Pallas kernels: 0 us -> 38.3 us
  waiting for transfers between devices: 26.2 us -> 0 us
  local copies, waits for them, and re-layouts: 21.8 us -> 2.99 us
  loops' own time: 4.04 us -> 0 us
  matrix products: 2.9 us -> 0 us
    pallas_call x0 -> x1, Pallas kernels: none -> 38.3 us  [local(): pl.pallas_call(functools.partial(body, n_gx, n_gy), out_shape=jax.ShapeDt...]
    ppermute x8 -> x0, starting transfers between devices: 37.2 us -> none  [the longest x4 29.2 us: extended(): lax.ppermute(lax.slice_in_dim(block, 0, width, axis=dim), axis, backward)]
    mul x49 -> x0, other arithmetic: 34.3 us -> none  [the longest x48 33.3 us: settle(): return (fall_k * settled, settled)]
    all_to_all x3 -> x0, waiting for transfers between devices: 24.6 us -> none  [the longest x1 9.62 us: local(): lax.all_to_all(tendency, 'gx', split_axis=0, concat_axis=0, tiled=True)]
    all_to_all x3 -> x0, starting transfers between devices: 18 us -> none  [the longest x1 9.7 us: local(): lax.all_to_all(sent_slots, 'gx', split_axis=0, concat_axis=0, tiled=True)]
    gather x6 -> x0, local copies, waits for them, and re-layouts: 6.11 us -> none  [the longest x1 1.53 us: local(): packed = flat_state[owner_order].reshape(peers, per_peer, row_width)]
    sort x2 -> x0, other arithmetic: 5.15 us -> none  [the longest x1 2.62 us: local(): inverse_order = jnp.argsort(owner_order)]
    another operation x3 -> x0, loops' own time: 4.04 us -> none  [the longest x1 1.64 us: physics(): lax.scan(backward, jnp.zeros_like(fields[0]), (gains, values), reverse=True)]
  transfers between devices with their start and end apart: 11 -> 0, of which waited for: 5 -> 0; matrix products, arithmetic and copies ran while one was open for 8% -> 0% of each run, Pallas kernels for 0% -> 0%
where the time goes in v1:
time: 41.5 us; the launch traced here: 41.3 us
  Pallas kernels  38.3 us (92%)
  local copies, waits for them, and re-layouts  2.99 us (7%)
    pallas_call x1, Pallas kernels, local(): pl.pallas_call(functools.partial(body, n_gx, n_gy), out_shape=jax.ShapeDt...  38.3 us
    unnamed x1, local copies, waits for them, and re-layouts  1.72 us
    reshape x1, local copies, waits for them, and re-layouts, local(): hyper.reshape(1, FLD)  1.27 us

profile of v1, /device:TPU:1, one launch (start us, length us, event | category | flops | bytes accessed | tf_op | source)
XLA Modules:
  0.0 41.3 jit_solution(4679570338276015887)
XLA Ops:
  0.0 1.3 %reshape.3.hyper = f32[1,528]{1,0:T(1,128)} reshape(f32[528]{0:T(1024)} %param.11) | data formatting | bytes 4224 | tf_op jit(solution)/shard_map/reshape | solution.py:348
  1.3 38.3 %shard_map.100 = f32[4,32,528]{2,1,0:T(8,128)} custom-call(f32[4,32,528]{2,1,0:T(8,128)} %state.1, f32[1,528]{1,0:T(1,128)} %reshape.3.hyper, f32[4,32]{1,0:T(4,128)} %pmass.1, f32[4,32]{1,0:T(4,128)} %imass.1, s32[4,32]{1,0:T(4,128)} %slots.1, f32[1,48,128]{2,1,0:T(8,128)} %vdiff.1, f32[1,48,128]{2,1,0:T(8,128)} %frate.1, f32[1,48,128]{2,1,0:T(8,128)} %cfrac.1, ...), custom_call_target="tpu_custom_call" | custom-call | tf_op jit(solution)/shard_map/pallas_call | solution.py:313
  39.6 1.7 %copy.12 = f32[4,32,528]{2,1,0:T(8,128)} copy(f32[4,32,528]{2,1,0:T(8,128)} %shard_map.100) | data formatting | bytes 540672

commit v2 on v1

v2 whole, which is shorter than its diff:
```python
import functools

import jax
import jax.numpy as jnp
import numpy as np
from jax import lax
from jax.experimental import pallas as pl
from jax.experimental.pallas import tpu as pltpu
from jax.sharding import PartitionSpec as P

MESH = pl.DeviceIdType.MESH
F32 = jnp.float32
BF16 = jnp.bfloat16
NX, NY, COLS, LEV, VARS = 4, 32, 128, 48, 11
FLD = LEV * VARS


def second_table():
    nodes = np.array([-1.0, -1.0 / np.sqrt(5.0), 1.0 / np.sqrt(5.0), 1.0])
    deriv = np.zeros((4, 4))
    for i in range(4):
        for j in range(4):
            if i == j:
                deriv[i, j] = sum(1.0 / (nodes[i] - nodes[o]) for o in range(4) if o != i)
            else:
                upper = np.prod([nodes[i] - nodes[o] for o in range(4) if o != i])
                lower = np.prod([nodes[j] - nodes[o] for o in range(4) if o != j])
                deriv[i, j] = upper / (lower * (nodes[i] - nodes[j]))
    return (deriv @ deriv).astype(np.float32)


def tables():
    second = second_table()
    x, y = np.divmod(np.arange(COLS), NY)
    same_x = x[:, None] == x[None, :]
    same_y = y[:, None] == y[None, :]
    same_e = (y[:, None] // 4) == (y[None, :] // 4)
    lap = np.where(same_y, second[x[:, None], x[None, :]], 0.0)
    lap = lap + np.where(same_x & same_e, second[y[:, None] % 4, y[None, :] % 4], 0.0)
    twin = np.where(y % 4 == 0, y - 1, np.where(y % 4 == 3, y + 1, -5))
    pick = np.eye(COLS) + np.where(same_x & (y[None, :] == twin[:, None]), 1.0, 0.0)
    edge = np.zeros((8, COLS))
    for i in range(4):
        edge[i, i * NY] = 1.0
        edge[4 + i, i * NY + NY - 1] = 1.0
    return lap.astype(np.float32), np.concatenate([pick, edge], 0).astype(np.float32)


def split(value):
    high = value.astype(BF16)
    return high, (value - high.astype(F32)).astype(BF16)


def dot(a, b):
    return jnp.dot(a, b, preferred_element_type=F32)


def exact(a, b, dims):
    return lax.dot_general(
        a, b, (dims, ((), ())), precision=lax.Precision.HIGHEST, preferred_element_type=F32
    )


def iota(shape, dim):
    return lax.broadcasted_iota(jnp.int32, shape, dim)


def body(
    n_gx, n_gy,
    state, hyper, pmass, imass, slots, vdiff, frate, cfrac, lap, pick,
    tr, fac,
    v, tsum, acc, edges, xin, yin, cin, small, sl, coef, sent, got, lap_s, pick_s, hyp, dyn,
    in_sem, hs_sem, hr_sem, gs_sem, gr_sem,
):
    per = COLS // n_gx
    half = per // 2
    me = lax.axis_index("gx")
    my = lax.axis_index("gy")
    left, right = lax.rem(me + n_gx - 1, n_gx), lax.rem(me + 1, n_gx)
    down, up = lax.rem(my + n_gy - 1, n_gy), lax.rem(my + 1, n_gy)
    peers = [lax.rem(me + i, n_gx) for i in range(1, n_gx)]
    around = [(left, my), (right, my), (me, down), (me, up),
              (left, down), (left, up), (right, down), (right, up)]

    loads = [
        pltpu.make_async_copy(vdiff.at[0], coef.at[pl.ds(0, LEV)], in_sem.at[0]),
        pltpu.make_async_copy(pmass, small.at[0], in_sem.at[1]),
        pltpu.make_async_copy(imass, small.at[1], in_sem.at[2]),
        pltpu.make_async_copy(lap, lap_s, in_sem.at[3]),
        pltpu.make_async_copy(pick, pick_s, in_sem.at[4]),
        pltpu.make_async_copy(state, v, in_sem.at[5]),
        pltpu.make_async_copy(slots, sl.at[me], in_sem.at[6]),
        pltpu.make_async_copy(frate.at[0], coef.at[pl.ds(2 * LEV, LEV)], in_sem.at[7]),
        pltpu.make_async_copy(cfrac.at[0], coef.at[pl.ds(3 * LEV, LEV)], in_sem.at[8]),
        pltpu.make_async_copy(hyper, hyp.at[0], in_sem.at[9]),
    ]
    for load in loads[1:6]:
        load.start()
    barrier = pltpu.get_barrier_semaphore()
    for target in around[4:] + around[2:4] + [(q, my) for q in peers]:
        pl.semaphore_signal(barrier, inc=1, device_id=target, device_id_type=MESH)
    for load in loads[:1] + loads[6:]:
        load.start()

    rows, lanes = iota((COLS, COLS), 0), iota((COLS, COLS), 1)
    tri = jnp.where(rows < lanes, 1.0, 0.0).astype(BF16)
    level = iota((LEV, COLS), 0)

    def as_row(block):
        return jnp.concatenate([block[x : x + 1, :] for x in range(NX)], axis=1)

    for load in loads[1:5]:
        load.wait()
    mass_row = as_row(small[0])
    inv_row = as_row(small[1])
    inv_col = jnp.sum(jnp.where(rows == lanes, inv_row, 0.0), axis=1, keepdims=True)
    op_high, op_low = split(exact(pick_s[...] * mass_row, lap_s[...], ((1,), (0,))))

    def weigh(r, field):
        high, low = split(field)
        total = dot(op_high, high) + (dot(op_high, low) + dot(op_low, high))
        tsum[r] = total[:COLS]
        for i in range(8):
            edges[r, i] = total[COLS + i : COLS + i + 1]

    def halo(r):
        plan = [
            (tsum.at[r, pl.ds(0, NY)], xin.at[r, 1]),
            (tsum.at[r, pl.ds(COLS - NY, NY)], xin.at[r, 0]),
            (edges.at[r, pl.ds(0, 4)], yin.at[r, 1]),
            (edges.at[r, pl.ds(4, 4)], yin.at[r, 0]),
            (edges.at[r, 0], cin.at[r, 3]),
            (edges.at[r, 4], cin.at[r, 2]),
            (edges.at[r, 3], cin.at[r, 1]),
            (edges.at[r, 7], cin.at[r, 0]),
        ]
        copies = [
            pltpu.make_async_remote_copy(
                src_ref=src, dst_ref=dst, send_sem=hs_sem.at[r, i], recv_sem=hr_sem.at[r, i],
                device_id=around[i], device_id_type=MESH,
            )
            for i, (src, dst) in enumerate(plan)
        ]
        for copy in copies[4:] + copies[2:4] + copies[:2]:
            copy.start()
        return copies

    def assemble(r):
        acc[pl.ds(0, NY), :] = tsum[r, pl.ds(0, NY)] + xin[r, 0]
        acc[pl.ds(NY, COLS - 2 * NY), :] = tsum[r, pl.ds(NY, COLS - 2 * NY)]
        acc[pl.ds(COLS - NY, NY), :] = tsum[r, pl.ds(COLS - NY, NY)] + xin[r, 1]
        corner = {0: (0, 1), 3: (2, 3)}
        for x in range(NX):
            low, high = yin[r, 0, x], yin[r, 1, x]
            if x in corner:
                low = low + cin[r, corner[x][0]]
                high = high + cin[r, corner[x][1]]
            acc[pl.ds(NY * x, 1), :] = acc[pl.ds(NY * x, 1), :] + low
            acc[pl.ds(NY * x + NY - 1, 1), :] = acc[pl.ds(NY * x + NY - 1, 1), :] + high
        return inv_col * acc[...]

    loads[5].wait()
    field = v[...].reshape(COLS, FLD)
    weigh(0, field)

    loads[0].wait()
    diff = coef[pl.ds(0, LEV), :]
    above = jnp.where(level == 0, 0.0, diff)
    below = jnp.where(level == LEV - 1, 0.0, pltpu.roll(diff, LEV - 1, 0))
    surface = jnp.where(level == LEV - 1, diff[0:1], 0.0)
    centre = 1.0 + above + below + surface
    gain = jnp.zeros((1, COLS), F32)
    for k in range(LEV):
        scale = 1.0 / (centre[k : k + 1] - above[k : k + 1] * gain)
        gain = below[k : k + 1] * scale
        coef[pl.ds(LEV + k, 1), :] = scale
    for load in loads[6:9]:
        load.wait()

    pl.semaphore_wait(barrier, n_gx - 1 + 6)

    def exchange(which, box, source):
        copies = [
            pltpu.make_async_remote_copy(
                src_ref=source(q), dst_ref=box.at[me],
                send_sem=gs_sem.at[which], recv_sem=gr_sem.at[which],
                device_id=(q, my), device_id_type=MESH,
            )
            for q in peers
        ]
        for copy in copies:
            copy.start()
        return pltpu.make_async_remote_copy(
            src_ref=box.at[pl.ds(0, n_gx - 1)], dst_ref=box.at[pl.ds(0, n_gx - 1)],
            send_sem=gs_sem.at[which], recv_sem=gr_sem.at[which],
            device_id=(right, my), device_id_type=MESH,
        )

    slot_all = exchange(0, sl, lambda q: sl.at[me])
    first = halo(0)

    own = as_row(sl[me])
    span = own // COLS
    member = jnp.where(span == iota((n_gx, COLS), 0), 1.0, 0.0)
    before = dot(member.astype(BF16), tri)
    rank = jnp.sum(member * before, axis=0, keepdims=True)
    place = span * per + rank.astype(jnp.int32)
    order = jnp.where(rows == place, 1.0, 0.0)
    pair = iota((COLS // 2, COLS), 0)
    pair = (pair // half) * per + pair % half
    order_two = jnp.concatenate(
        [jnp.where(pair == place, 1.0, 0.0), jnp.where(pair + half == place, 1.0, 0.0)], axis=0
    )

    spread = jnp.where(
        iota((COLS, n_gx), 0) // per == iota((COLS, n_gx), 1), 1.0, 0.0
    ).astype(BF16)
    table = coef[...]
    late = table[COLS:].T
    main = table[:COLS].T
    blank = jnp.zeros((COLS, 4 * LEV - COLS), F32)
    rest = jnp.concatenate(
        [jnp.concatenate([late, blank], axis=1), jnp.concatenate([blank, late], axis=1)], axis=0
    )
    slot_all.wait_recv()
    every = jnp.concatenate([sl[:, x, :] for x in range(NX)], axis=1)
    mine = (every // COLS) == me
    before = dot(jnp.where(mine, 1.0, 0.0).astype(BF16), tri)
    ranked = jnp.where(mine, before, -1.0).astype(BF16)
    within = (every % COLS).astype(F32).astype(BF16)
    hit = dot(spread, ranked) == (rows % per).astype(F32)
    chosen = jnp.sum(jnp.where(hit, dot(spread, within), 0.0), axis=1, keepdims=True)
    onehot = jnp.where(chosen == lanes.astype(F32), 1.0, 0.0)
    sent[:, pl.ds(0, per), :] = exact(onehot, main, ((1,), (0,))).reshape(n_gx, per, COLS)
    halves = onehot.reshape(n_gx, 2, half, COLS)
    halves = jnp.concatenate(
        [halves[:, i].reshape(COLS // 2, COLS) for i in range(2)], axis=1
    )
    sent[:, pl.ds(per, half), :] = exact(halves, rest, ((1,), (0,))).reshape(n_gx, half, COLS)
    coef_all = exchange(1, got, lambda q: sent.at[q])
    got[me] = sent[me]

    for copy in first:
        copy.wait_recv()
    weigh(1, assemble(0))
    second = halo(1)

    coef_all.wait_recv()
    box = got[:, pl.ds(0, per), :].reshape(COLS, COLS)
    tail = got[:, pl.ds(per, half), :].reshape(COLS // 2, COLS)
    wide = COLS // 2
    tail = jnp.concatenate([tail[:, :wide], tail[:, wide:]], axis=0)
    early = exact(box, order, ((0,), (0,)))
    late = exact(tail, order_two, ((0,), (0,)))
    diff, scale = early[:LEV], early[LEV : 2 * LEV]
    fall = jnp.concatenate([early[2 * LEV :], late[: 3 * LEV - COLS]], axis=0)
    cloud = late[3 * LEV - COLS :]
    fac[0] = jnp.where(level == 0, 0.0, diff) * scale
    fac[1] = jnp.where(level == LEV - 1, 0.0, pltpu.roll(diff, LEV - 1, 0)) * scale
    fac[2] = scale
    settle = 1.0 / (1.0 + fall)
    fac[3] = settle
    fac[4] = jnp.where(level == 0, 0.0, pltpu.roll(fall, 1, 0)) * settle
    fac[5] = cloud * 0.5

    loads[9].wait()
    for copy in second:
        copy.wait_recv()
    dyn[:, pl.ds(0, FLD)] = v[...].reshape(COLS, FLD) - hyp[...] * assemble(1)
    for j in range(5):
        tr[pl.ds(COLS * j, COLS), :] = dyn[:, pl.ds(COLS * j, COLS)].T
    slot_all.wait_send()
    coef_all.wait_send()
    for copy in first + second:
        copy.wait_send()


def columns(tin, fac, out, tr, wk, rain, res, sem):
    def strided(k):
        return pl.ds(k, VARS, stride=LEV)

    value = jnp.zeros((VARS, COLS), F32)
    for k in range(LEV):
        value = tin[strided(k), :] * fac[2, pl.ds(k, 1), :] + fac[0, pl.ds(k, 1), :] * value
        wk[k] = value
    value = jnp.zeros((VARS, COLS), F32)
    for k in reversed(range(LEV)):
        value = wk[k] + fac[1, pl.ds(k, 1), :] * value
        tr[strided(k), :] = value

    heat, vapour, liquid = (tr[pl.ds(LEV * j, LEV), :] for j in range(3))
    moved = fac[5] * jnp.maximum(vapour - 0.3 * heat, 0.0)
    tr[pl.ds(0, LEV), :] = heat + 2.0 * moved
    tr[pl.ds(LEV, LEV), :] = vapour - moved
    rain[...] = (liquid + moved) * fac[3]
    drop = jnp.zeros((1, COLS), F32)
    for k in range(LEV):
        drop = rain[pl.ds(k, 1), :] + fac[4, pl.ds(k, 1), :] * drop
        tr[pl.ds(2 * LEV + k, 1), :] = drop

    for j in range(5):
        width = min(COLS, FLD - COLS * j)
        part = tr[pl.ds(COLS * j, COLS), :].T[:, :width].reshape(NX, NY, width)
        res[:, :, pl.ds(COLS * j, width)] = part
    store = pltpu.make_async_copy(res, out, sem)
    store.start()
    store.wait()


def solution(mesh):
    n_gx, n_gy = mesh.shape["gx"], mesh.shape["gy"]
    per = COLS // n_gx
    lap, pick = tables()
    anywhere = pl.BlockSpec(memory_space=pl.ANY)
    inside = pl.BlockSpec(memory_space=pltpu.VMEM)
    dma = pltpu.SemaphoreType.DMA

    def local(state, hyper, pmass, imass, slots, vdiff, frate, cfrac):
        fields, factors = pl.pallas_call(
            functools.partial(body, n_gx, n_gy),
            out_shape=(pltpu.VMEM((5 * COLS, COLS), F32), pltpu.VMEM((6, LEV, COLS), F32)),
            in_specs=[anywhere] * 10,
            out_specs=(inside, inside),
            scratch_shapes=[
                pltpu.VMEM((NX, NY, FLD), F32),
                pltpu.VMEM((2, COLS, FLD), F32),
                pltpu.VMEM((COLS, FLD), F32),
                pltpu.VMEM((2, 8, 1, FLD), F32),
                pltpu.VMEM((2, 2, NY, FLD), F32),
                pltpu.VMEM((2, 2, 4, 1, FLD), F32),
                pltpu.VMEM((2, 4, 1, FLD), F32),
                pltpu.VMEM((2, NX, NY), F32),
                pltpu.VMEM((n_gx, NX, NY), jnp.int32),
                pltpu.VMEM((4 * LEV, COLS), F32),
                pltpu.VMEM((n_gx, per + per // 2, COLS), F32),
                pltpu.VMEM((n_gx, per + per // 2, COLS), F32),
                pltpu.VMEM((COLS, COLS), F32),
                pltpu.VMEM((COLS + 8, COLS), F32),
                pltpu.VMEM((1, FLD), F32),
                pltpu.VMEM((COLS, 5 * COLS), F32),
                dma((10,)),
                dma((2, 8)),
                dma((2, 8)),
                dma((2,)),
                dma((2,)),
            ],
            compiler_params=pltpu.CompilerParams(collective_id=0, has_side_effects=True),
        )(state, hyper, pmass, imass, slots, vdiff, frate, cfrac,
          jnp.asarray(lap), jnp.asarray(pick))
        return pl.pallas_call(
            columns,
            out_shape=jax.ShapeDtypeStruct((NX, NY, FLD), F32),
            in_specs=[inside, inside],
            out_specs=anywhere,
            scratch_shapes=[
                pltpu.VMEM((5 * COLS, COLS), F32),
                pltpu.VMEM((LEV, VARS, COLS), F32),
                pltpu.VMEM((LEV, COLS), F32),
                pltpu.VMEM((NX, NY, FLD), F32),
                dma,
            ],
        )(*(pltpu.with_memory_space_constraint(x, pltpu.VMEM) for x in (fields, factors)))

    placed = (
        P("gx", "gy", None), P(), P("gx", "gy"), P("gx", "gy"), P("gx", "gy"),
        P("gy", None, "gx"), P("gy", None, "gx"), P("gy", None, "gx"),
    )
    return jax.shard_map(
        local, mesh=mesh, in_specs=placed, out_specs=P("gx", "gy", None), check_vma=False
    )
```

time: 41.5 us -> 36.7 us (0.88)
  local copies, waits for them, and re-layouts: 2.99 us -> 0 us
  Pallas kernels: 38.3 us -> 36.5 us
    pallas_call x1 -> x2, Pallas kernels: 38.3 us -> 36.5 us  [the longest x1 35.3 us: local(): pl.pallas_call(functools.partial(body, n_gx, n_gy), out_shape=(pltpu.VMEM...]
    unnamed x1 -> x0, local copies, waits for them, and re-layouts: 1.72 us -> none
    reshape x1 -> x0, local copies, waits for them, and re-layouts: 1.27 us -> none  [local(): hyper.reshape(1, FLD)]
where the time goes in v2:
time: 36.7 us; the launch traced here: 36.5 us
  Pallas kernels  36.5 us (99%)
    pallas_call x1, Pallas kernels, local(): pl.pallas_call(functools.partial(body, n_gx, n_gy), out_shape=(pltpu.VMEM...  35.3 us
    pallas_call x1, Pallas kernels, local(): pl.pallas_call(columns, out_shape=jax.ShapeDtypeStruct((NX, NY, FLD), F32...  1.22 us

profile of v2, /device:TPU:1, one launch (start us, length us, event | category | flops | bytes accessed | tf_op | source)
XLA Modules:
  0.0 36.5 jit_solution(4367598600915909543)
XLA Ops:
  0.0 35.3 %shard_map.100 = (f32[640,128]{1,0:T(8,128)S(1)}, f32[6,48,128]{2,1,0:T(8,128)S(1)}) custom-call(f32[4,32,528]{2,1,0:T(8,128)} %state.1, f32[528]{0:T(1024)} %hyper.1, f32[4,32]{1,0:T(4,128)} %pmass.1, f32[4,32]{1,0:T(4,128)} %imass.1, s32[4,32]{1,0:T(4,128)} %slots.1, f32[1,48,128]{2,1,0:T(8,128)} %vdiff.1, f32[1,48,128]{2,1,0:T(8,128)} %frate.1, ...), custom_call_target="tpu_custom_call" | custom-call | tf_op jit(solution)/shard_map/pallas_call | solution.py:319
  35.3 1.2 %shard_map.101 = f32[4,32,528]{2,1,0:T(8,128)} custom-call(f32[640,128]{1,0:T(8,128)S(1)} %get-tuple-element.7.tin, f32[6,48,128]{2,1,0:T(8,128)S(1)} %get-tuple-element.8.fac), custom_call_target="tpu_custom_call" | custom-call | tf_op jit(solution)/shard_map/pallas_call | solution.py:350

commit v3 on v2

--- a/solution.py
+++ b/solution.py
@@ -12,6 +12,7 @@
 F32 = jnp.float32
 BF16 = jnp.bfloat16
 NX, NY, COLS, LEV, VARS = 4, 32, 128, 48, 11
+Z = 8
 FLD = LEV * VARS
 
 
@@ -70,7 +71,7 @@
     state, hyper, pmass, imass, slots, vdiff, frate, cfrac, lap, pick,
     tr, fac,
     v, tsum, acc, edges, xin, yin, cin, small, sl, coef, sent, got, lap_s, pick_s, hyp, dyn,
-    in_sem, hs_sem, hr_sem, gs_sem, gr_sem,
+    in_sem, hs_sem, hr_sem, gs_sem, gr_sem, here_sem,
 ):
     per = COLS // n_gx
     half = per // 2
@@ -78,7 +79,11 @@
     my = lax.axis_index("gy")
     left, right = lax.rem(me + n_gx - 1, n_gx), lax.rem(me + 1, n_gx)
     down, up = lax.rem(my + n_gy - 1, n_gy), lax.rem(my + 1, n_gy)
-    peers = [lax.rem(me + i, n_gx) for i in range(1, n_gx)]
+    far_first = sorted(range(1, n_gx), key=lambda i: -min(i, n_gx - i))
+    peers = [lax.rem(me + i, n_gx) for i in far_first]
+    core = lax.rem(me, 2)
+    chip = me // 2
+    beside = lax.rem(chip + n_gx // 2 - 1 + 2 * core, n_gx // 2)
     around = [(left, my), (right, my), (me, down), (me, up),
               (left, down), (left, up), (right, down), (right, up)]
 
@@ -97,8 +102,39 @@
     for load in loads[1:6]:
         load.start()
     barrier = pltpu.get_barrier_semaphore()
-    for target in around[4:] + around[2:4] + [(q, my) for q in peers]:
-        pl.semaphore_signal(barrier, inc=1, device_id=target, device_id_type=MESH)
+
+    def arrive(gx, gy):
+        pl.semaphore_signal(barrier, inc=1, device_id=(gx, gy), device_id_type=MESH)
+
+    for gy in (down, up):
+        arrive(2 * beside + 1, gy)
+        arrive(2 * chip + 1, gy)
+    arrive(2 * beside + 1, my)
+    for i in sorted(range(1, n_gx // 2), key=lambda i: -min(i, n_gx // 2 - i)):
+        arrive(2 * lax.rem(chip + i, n_gx // 2), my)
+
+    @pl.when(core == 0)
+    def _():
+        arrive(me + 1, my)
+
+    @pl.when(core == 1)
+    def _():
+        arrive(me - 1, my)
+
+    def ready(counter, amount):
+        partner = me + 1 - 2 * core
+
+        @pl.when(core == counter)
+        def _():
+            pl.semaphore_wait(barrier, amount)
+            pl.semaphore_signal(
+                here_sem.at[counter], inc=1, device_id=(partner, my), device_id_type=MESH
+            )
+
+        @pl.when(core != counter)
+        def _():
+            pl.semaphore_wait(here_sem.at[counter], 1)
+
     for load in loads[:1] + loads[6:]:
         load.start()
 
@@ -141,9 +177,11 @@
             )
             for i, (src, dst) in enumerate(plan)
         ]
+        return copies
+
+    def begin(copies):
         for copy in copies[4:] + copies[2:4] + copies[:2]:
             copy.start()
-        return copies
 
     def assemble(r):
         acc[pl.ds(0, NY), :] = tsum[r, pl.ds(0, NY)] + xin[r, 0]
@@ -163,21 +201,7 @@
     field = v[...].reshape(COLS, FLD)
     weigh(0, field)
 
-    loads[0].wait()
-    diff = coef[pl.ds(0, LEV), :]
-    above = jnp.where(level == 0, 0.0, diff)
-    below = jnp.where(level == LEV - 1, 0.0, pltpu.roll(diff, LEV - 1, 0))
-    surface = jnp.where(level == LEV - 1, diff[0:1], 0.0)
-    centre = 1.0 + above + below + surface
-    gain = jnp.zeros((1, COLS), F32)
-    for k in range(LEV):
-        scale = 1.0 / (centre[k : k + 1] - above[k : k + 1] * gain)
-        gain = below[k : k + 1] * scale
-        coef[pl.ds(LEV + k, 1), :] = scale
-    for load in loads[6:9]:
-        load.wait()
-
-    pl.semaphore_wait(barrier, n_gx - 1 + 6)
+    first, second = halo(0), halo(1)
 
     def exchange(which, box, source):
         copies = [
@@ -188,16 +212,96 @@
             )
             for q in peers
         ]
-        for copy in copies:
-            copy.start()
-        return pltpu.make_async_remote_copy(
+        every = pltpu.make_async_remote_copy(
             src_ref=box.at[pl.ds(0, n_gx - 1)], dst_ref=box.at[pl.ds(0, n_gx - 1)],
             send_sem=gs_sem.at[which], recv_sem=gr_sem.at[which],
             device_id=(right, my), device_id_type=MESH,
         )
-
-    slot_all = exchange(0, sl, lambda q: sl.at[me])
-    first = halo(0)
+        return copies, every
+
+    slot_sends, slot_all = exchange(0, sl, lambda q: sl.at[me])
+    coef_sends, coef_all = exchange(1, got, lambda q: sent.at[q])
+
+    def pivots():
+        diff = coef[pl.ds(0, LEV), :]
+        above = jnp.where(level == 0, 0.0, diff)
+        below = jnp.where(level == LEV - 1, 0.0, pltpu.roll(diff, LEV - 1, 0))
+        surface = jnp.where(level == LEV - 1, diff[0:1], 0.0)
+        centre = 1.0 + above + below + surface
+        gain = jnp.zeros((1, COLS), F32)
+        for k in range(LEV):
+            scale = 1.0 / (centre[k : k + 1] - above[k : k + 1] * gain)
+            gain = below[k : k + 1] * scale
+            coef[pl.ds(LEV + k, 1), :] = scale
+
+    def ask():
+        ready(0, n_gx - 1)
+        for copy in slot_sends:
+            copy.start()
+
+    def answer():
+        spread = jnp.where(
+            iota((COLS, n_gx), 0) // per == iota((COLS, n_gx), 1), 1.0, 0.0
+        ).astype(BF16)
+        table = coef[...]
+        late = table[COLS:].T
+        main = table[:COLS].T
+        blank = jnp.zeros((COLS, 4 * LEV - COLS), F32)
+        rest = jnp.concatenate(
+            [jnp.concatenate([late, blank], axis=1), jnp.concatenate([blank, late], axis=1)],
+            axis=0,
+        )
+        slot_all.wait_recv()
+        every = jnp.concatenate([sl[:, x, :] for x in range(NX)], axis=1)
+        mine = (every // COLS) == me
+        before = dot(jnp.where(mine, 1.0, 0.0).astype(BF16), tri)
+        ranked = jnp.where(mine, before, -1.0).astype(BF16)
+        within = (every % COLS).astype(F32).astype(BF16)
+        hit = dot(spread, ranked) == (rows % per).astype(F32)
+        chosen = jnp.sum(jnp.where(hit, dot(spread, within), 0.0), axis=1, keepdims=True)
+        onehot = jnp.where(chosen == lanes.astype(F32), 1.0, 0.0)
+        sent[:, pl.ds(0, per), :] = exact(onehot, main, ((1,), (0,))).reshape(n_gx, per, COLS)
+        halves = onehot.reshape(n_gx, 2, half, COLS)
+        halves = jnp.concatenate(
+            [halves[:, i].reshape(COLS // 2, COLS) for i in range(2)], axis=1
+        )
+        sent[:, pl.ds(per, half), :] = exact(halves, rest, ((1,), (0,))).reshape(n_gx, half, COLS)
+        for copy in coef_sends:
+            copy.start()
+        got[me] = sent[me]
+
+    def pass_edges():
+        ready(1, 11)
+        begin(first)
+
+    def pass_again():
+        for copy in first:
+            copy.wait_recv()
+        weigh(1, assemble(0))
+        begin(second)
+
+    for load in loads[:1] + loads[6:9]:
+        load.wait()
+    early = lax.rem(my, Z) < 2
+
+    @pl.when(early)
+    def _():
+        pivots()
+        ask()
+        answer()
+
+    pass_edges()
+
+    @pl.when(jnp.logical_not(early))
+    def _():
+        pivots()
+        ask()
+
+    pass_again()
+
+    @pl.when(jnp.logical_not(early))
+    def _():
+        answer()
 
     own = as_row(sl[me])
     span = own // COLS
@@ -211,39 +315,6 @@
     order_two = jnp.concatenate(
         [jnp.where(pair == place, 1.0, 0.0), jnp.where(pair + half == place, 1.0, 0.0)], axis=0
     )
-
-    spread = jnp.where(
-        iota((COLS, n_gx), 0) // per == iota((COLS, n_gx), 1), 1.0, 0.0
-    ).astype(BF16)
-    table = coef[...]
-    late = table[COLS:].T
-    main = table[:COLS].T
-    blank = jnp.zeros((COLS, 4 * LEV - COLS), F32)
-    rest = jnp.concatenate(
-        [jnp.concatenate([late, blank], axis=1), jnp.concatenate([blank, late], axis=1)], axis=0
-    )
-    slot_all.wait_recv()
-    every = jnp.concatenate([sl[:, x, :] for x in range(NX)], axis=1)
-    mine = (every // COLS) == me
-    before = dot(jnp.where(mine, 1.0, 0.0).astype(BF16), tri)
-    ranked = jnp.where(mine, before, -1.0).astype(BF16)
-    within = (every % COLS).astype(F32).astype(BF16)
-    hit = dot(spread, ranked) == (rows % per).astype(F32)
-    chosen = jnp.sum(jnp.where(hit, dot(spread, within), 0.0), axis=1, keepdims=True)
-    onehot = jnp.where(chosen == lanes.astype(F32), 1.0, 0.0)
-    sent[:, pl.ds(0, per), :] = exact(onehot, main, ((1,), (0,))).reshape(n_gx, per, COLS)
-    halves = onehot.reshape(n_gx, 2, half, COLS)
-    halves = jnp.concatenate(
-        [halves[:, i].reshape(COLS // 2, COLS) for i in range(2)], axis=1
-    )
-    sent[:, pl.ds(per, half), :] = exact(halves, rest, ((1,), (0,))).reshape(n_gx, half, COLS)
-    coef_all = exchange(1, got, lambda q: sent.at[q])
-    got[me] = sent[me]
-
-    for copy in first:
-        copy.wait_recv()
-    weigh(1, assemble(0))
-    second = halo(1)
 
     coef_all.wait_recv()
     box = got[:, pl.ds(0, per), :].reshape(COLS, COLS)
@@ -343,6 +414,7 @@
                 dma((2, 8)),
                 dma((2,)),
                 dma((2,)),
+                pltpu.SemaphoreType.REGULAR((2,)),
             ],
             compiler_params=pltpu.CompilerParams(collective_id=0, has_side_effects=True),
         )(state, hyper, pmass, imass, slots, vdiff, frate, cfrac,

time: 36.7 us -> 36.2 us (0.986)
  Pallas kernels: 36.5 us -> 36 us
    pallas_call x1, Pallas kernels: 35.3 us -> 34.8 us  [local(): pl.pallas_call(functools.partial(body, n_gx, n_gy), out_shape=(pltpu.VMEM...]
where the time goes in v3:
time: 36.2 us; the launch traced here: 36 us
  Pallas kernels  36 us (99%)
    pallas_call x1, Pallas kernels, local(): pl.pallas_call(functools.partial(body, n_gx, n_gy), out_shape=(pltpu.VMEM...  34.8 us
    pallas_call x1, Pallas kernels, local(): pl.pallas_call(columns, out_shape=jax.ShapeDtypeStruct((NX, NY, FLD), F32...  1.22 us

profile of v3, /device:TPU:1, one launch (start us, length us, event | category | flops | bytes accessed | tf_op | source)
XLA Modules:
  0.0 36.0 jit_solution(111855328816593844)
XLA Ops:
  0.0 34.8 %shard_map.100 = (f32[640,128]{1,0:T(8,128)S(1)}, f32[6,48,128]{2,1,0:T(8,128)S(1)}) custom-call(f32[4,32,528]{2,1,0:T(8,128)} %state.1, f32[528]{0:T(1024)} %hyper.1, f32[4,32]{1,0:T(4,128)} %pmass.1, f32[4,32]{1,0:T(4,128)} %imass.1, s32[4,32]{1,0:T(4,128)} %slots.1, f32[1,48,128]{2,1,0:T(8,128)} %vdiff.1, f32[1,48,128]{2,1,0:T(8,128)} %frate.1, ...), custom_call_target="tpu_custom_call" | custom-call | tf_op jit(solution)/shard_map/pallas_call | solution.py:390
  34.8 1.2 %shard_map.101 = f32[4,32,528]{2,1,0:T(8,128)} custom-call(f32[640,128]{1,0:T(8,128)S(1)} %get-tuple-element.7.tin, f32[6,48,128]{2,1,0:T(8,128)S(1)} %get-tuple-element.8.fac), custom_call_target="tpu_custom_call" | custom-call | tf_op jit(solution)/shard_map/pallas_call | solution.py:422

commit v4 on v3

--- a/solution.py
+++ b/solution.py
@@ -150,11 +150,20 @@
     mass_row = as_row(small[0])
     inv_row = as_row(small[1])
     inv_col = jnp.sum(jnp.where(rows == lanes, inv_row, 0.0), axis=1, keepdims=True)
-    op_high, op_low = split(exact(pick_s[...] * mass_row, lap_s[...], ((1,), (0,))))
+    pick_high, pick_low = split(pick_s[...] * mass_row)
+    lap_high, lap_low = split(lap_s[...])
+    op_high, op_low = split(
+        dot(
+            jnp.concatenate([pick_high, pick_high], axis=1),
+            jnp.concatenate([lap_high, lap_low], axis=0),
+        )
+        + dot(pick_low, lap_high)
+    )
+    op_twice = jnp.concatenate([op_high, op_high], axis=1)
 
     def weigh(r, field):
         high, low = split(field)
-        total = dot(op_high, high) + (dot(op_high, low) + dot(op_low, high))
+        total = dot(op_twice, jnp.concatenate([high, low], axis=0)) + dot(op_low, high)
         tsum[r] = total[:COLS]
         for i in range(8):
             edges[r, i] = total[COLS + i : COLS + i + 1]
@@ -288,9 +297,12 @@
     def _():
         pivots()
         ask()
+
+    pass_edges()
+
+    @pl.when(early)
+    def _():
         answer()
-
-    pass_edges()
 
     @pl.when(jnp.logical_not(early))
     def _():

time: 36.2 us -> 34.5 us (0.953)
  the two profiles are of different devices: /device:TPU:1 before, /device:TPU:7 now
where the time goes in v4:
time: 34.5 us; the launch traced here: 34.4 us
  Pallas kernels  34.4 us (100%)
    pallas_call x1, Pallas kernels, local(): pl.pallas_call(functools.partial(body, n_gx, n_gy), out_shape=(pltpu.VMEM...  33.2 us
    pallas_call x1, Pallas kernels, local(): pl.pallas_call(columns, out_shape=jax.ShapeDtypeStruct((NX, NY, FLD), F32...  1.22 us

profile of v4, /device:TPU:7, one launch (start us, length us, event | category | flops | bytes accessed | tf_op | source)
XLA Modules:
  0.0 34.4 jit_solution(17278339809873203989)
XLA Ops:
  0.0 33.2 %shard_map.100 = (f32[640,128]{1,0:T(8,128)S(1)}, f32[6,48,128]{2,1,0:T(8,128)S(1)}) custom-call(f32[4,32,528]{2,1,0:T(8,128)} %state.1, f32[528]{0:T(1024)} %hyper.1, f32[4,32]{1,0:T(4,128)} %pmass.1, f32[4,32]{1,0:T(4,128)} %imass.1, s32[4,32]{1,0:T(4,128)} %slots.1, f32[1,48,128]{2,1,0:T(8,128)} %vdiff.1, f32[1,48,128]{2,1,0:T(8,128)} %frate.1, ...), custom_call_target="tpu_custom_call" | custom-call | tf_op jit(solution)/shard_map/pallas_call | solution.py:402
  33.2 1.2 %shard_map.101 = f32[4,32,528]{2,1,0:T(8,128)} custom-call(f32[640,128]{1,0:T(8,128)S(1)} %get-tuple-element.7.tin, f32[6,48,128]{2,1,0:T(8,128)S(1)} %get-tuple-element.8.fac), custom_call_target="tpu_custom_call" | custom-call | tf_op jit(solution)/shard_map/pallas_call | solution.py:434

commit v5 on v4

--- a/solution.py
+++ b/solution.py
@@ -13,6 +13,8 @@
 BF16 = jnp.bfloat16
 NX, NY, COLS, LEV, VARS = 4, 32, 128, 48, 11
 Z = 8
+RUN = 8
+RUNS = LEV // RUN
 FLD = LEV * VARS
 
 
@@ -99,7 +101,7 @@
         pltpu.make_async_copy(cfrac.at[0], coef.at[pl.ds(3 * LEV, LEV)], in_sem.at[8]),
         pltpu.make_async_copy(hyper, hyp.at[0], in_sem.at[9]),
     ]
-    for load in loads[1:6]:
+    for load in loads[5:6] + loads[1:5]:
         load.start()
     barrier = pltpu.get_barrier_semaphore()
 
@@ -161,12 +163,27 @@
     )
     op_twice = jnp.concatenate([op_high, op_high], axis=1)
 
-    def weigh(r, field):
+    def first_rows(op):
+        return jnp.concatenate([op[COLS:], op[:NY], op[COLS - NY : COLS]], axis=0)
+
+    border_twice, border_low = first_rows(op_twice), first_rows(op_low)
+
+    def weigh(r, field, copies):
         high, low = split(field)
-        total = dot(op_twice, jnp.concatenate([high, low], axis=0)) + dot(op_low, high)
-        tsum[r] = total[:COLS]
+        both = jnp.concatenate([high, low], axis=0)
+        border = dot(border_twice, both) + dot(border_low, high)
         for i in range(8):
-            edges[r, i] = total[COLS + i : COLS + i + 1]
+            edges[r, i] = border[i : i + 1]
+        tsum[r, pl.ds(0, NY)] = border[8 : 8 + NY]
+        tsum[r, pl.ds(COLS - NY, NY)] = border[8 + NY :]
+        if r == 0:
+            ready(1, 11)
+        for copy in copies[4:] + copies[2:4] + copies[:2]:
+            copy.start()
+        middle = slice(NY, COLS - NY)
+        tsum[r, pl.ds(NY, COLS - 2 * NY)] = dot(op_twice[middle], both) + dot(op_low[middle], high)
+
+    kind = [0, 0, 1, 1, 2, 2, 2, 2]
 
     def halo(r):
         plan = [
@@ -181,16 +198,20 @@
         ]
         copies = [
             pltpu.make_async_remote_copy(
-                src_ref=src, dst_ref=dst, send_sem=hs_sem.at[r, i], recv_sem=hr_sem.at[r, i],
+                src_ref=src, dst_ref=dst, send_sem=hs_sem.at[r, kind[i]], recv_sem=hr_sem.at[r, kind[i]],
                 device_id=around[i], device_id_type=MESH,
             )
             for i, (src, dst) in enumerate(plan)
         ]
-        return copies
-
-    def begin(copies):
-        for copy in copies[4:] + copies[2:4] + copies[:2]:
-            copy.start()
+        whole = [
+            pltpu.make_async_remote_copy(
+                src_ref=box.at[r], dst_ref=box.at[r],
+                send_sem=hs_sem.at[r, i], recv_sem=hr_sem.at[r, i],
+                device_id=(right, my), device_id_type=MESH,
+            )
+            for i, box in enumerate((xin, yin, cin))
+        ]
+        return copies, whole
 
     def assemble(r):
         acc[pl.ds(0, NY), :] = tsum[r, pl.ds(0, NY)] + xin[r, 0]
@@ -206,11 +227,7 @@
             acc[pl.ds(NY * x + NY - 1, 1), :] = acc[pl.ds(NY * x + NY - 1, 1), :] + high
         return inv_col * acc[...]
 
-    loads[5].wait()
-    field = v[...].reshape(COLS, FLD)
-    weigh(0, field)
-
-    first, second = halo(0), halo(1)
+    (first, first_all), (second, second_all) = halo(0), halo(1)
 
     def exchange(which, box, source):
         copies = [
@@ -232,6 +249,8 @@
     coef_sends, coef_all = exchange(1, got, lambda q: sent.at[q])
 
     def pivots():
+        for load in loads[:1] + loads[7:9]:
+            load.wait()
         diff = coef[pl.ds(0, LEV), :]
         above = jnp.where(level == 0, 0.0, diff)
         below = jnp.where(level == LEV - 1, 0.0, pltpu.roll(diff, LEV - 1, 0))
@@ -244,6 +263,7 @@
             coef[pl.ds(LEV + k, 1), :] = scale
 
     def ask():
+        loads[6].wait()
         ready(0, n_gx - 1)
         for copy in slot_sends:
             copy.start()
@@ -280,17 +300,14 @@
         got[me] = sent[me]
 
     def pass_edges():
-        ready(1, 11)
-        begin(first)
+        loads[5].wait()
+        weigh(0, v[...].reshape(COLS, FLD), first)
 
     def pass_again():
-        for copy in first:
+        for copy in first_all:
             copy.wait_recv()
-        weigh(1, assemble(0))
-        begin(second)
-
-    for load in loads[:1] + loads[6:9]:
-        load.wait()
+        weigh(1, assemble(0), second)
+
     early = lax.rem(my, Z) < 2
 
     @pl.when(early)
@@ -345,16 +362,25 @@
     fac[3] = settle
     fac[4] = jnp.where(level == 0, 0.0, pltpu.roll(fall, 1, 0)) * settle
     fac[5] = cloud * 0.5
+    for source, target, steps in (
+        (0, 6, range(RUN)), (1, 7, reversed(range(RUN))), (4, 8, range(RUN))
+    ):
+        product = None
+        for i in steps:
+            at = pl.ds(i, RUNS, stride=RUN)
+            term = fac[source, at, :]
+            product = term if product is None else product * term
+            fac[target, at, :] = product
 
     loads[9].wait()
-    for copy in second:
+    for copy in second_all:
         copy.wait_recv()
     dyn[:, pl.ds(0, FLD)] = v[...].reshape(COLS, FLD) - hyp[...] * assemble(1)
     for j in range(5):
         tr[pl.ds(COLS * j, COLS), :] = dyn[:, pl.ds(COLS * j, COLS)].T
     slot_all.wait_send()
     coef_all.wait_send()
-    for copy in first + second:
+    for copy in first_all + second_all:
         copy.wait_send()
 
 
@@ -362,32 +388,66 @@
     def strided(k):
         return pl.ds(k, VARS, stride=LEV)
 
-    value = jnp.zeros((VARS, COLS), F32)
+    def row(which, k):
+        return fac[which, pl.ds(k, 1), :]
+
+    value = [None] * RUNS
+    for i in range(RUN):
+        for r in range(RUNS):
+            k = RUN * r + i
+            term = tin[strided(k), :] * row(2, k)
+            value[r] = term if i == 0 else term + row(0, k) * value[r]
+            wk[k] = value[r]
+    for r in range(1, RUNS):
+        value[r] = value[r] + row(6, RUN * r + RUN - 1) * value[r - 1]
+    ends, value = value, [None] * RUNS
+    for i in reversed(range(RUN)):
+        for r in range(RUNS):
+            k = RUN * r + i
+            term = wk[k] if r == 0 else wk[k] + row(6, k) * ends[r - 1]
+            value[r] = term if i == RUN - 1 else term + row(1, k) * value[r]
+            wk[k] = value[r]
+    for r in reversed(range(RUNS - 1)):
+        value[r] = value[r] + row(7, RUN * r) * value[r + 1]
     for k in range(LEV):
-        value = tin[strided(k), :] * fac[2, pl.ds(k, 1), :] + fac[0, pl.ds(k, 1), :] * value
-        wk[k] = value
-    value = jnp.zeros((VARS, COLS), F32)
-    for k in reversed(range(LEV)):
-        value = wk[k] + fac[1, pl.ds(k, 1), :] * value
-        tr[strided(k), :] = value
+        r = k // RUN
+        tr[strided(k), :] = wk[k] if r == RUNS - 1 else wk[k] + row(7, k) * value[r + 1]
+
+    def emit(j):
+        width = min(COLS, FLD - COLS * j)
+        part = tr[pl.ds(COLS * j, COLS), :].T[:, :width].reshape(NX, NY, width)
+        res[:, :, pl.ds(COLS * j, width)] = part
+
+    for j in (2, 3, 4):
+        emit(j)
+    high = pl.ds(2 * COLS, FLD - 2 * COLS)
+    stores = [pltpu.make_async_copy(res.at[:, :, high], out.at[:, :, high], sem.at[0])]
+    stores[0].start()
 
     heat, vapour, liquid = (tr[pl.ds(LEV * j, LEV), :] for j in range(3))
     moved = fac[5] * jnp.maximum(vapour - 0.3 * heat, 0.0)
     tr[pl.ds(0, LEV), :] = heat + 2.0 * moved
     tr[pl.ds(LEV, LEV), :] = vapour - moved
     rain[...] = (liquid + moved) * fac[3]
-    drop = jnp.zeros((1, COLS), F32)
-    for k in range(LEV):
-        drop = rain[pl.ds(k, 1), :] + fac[4, pl.ds(k, 1), :] * drop
-        tr[pl.ds(2 * LEV + k, 1), :] = drop
-
-    for j in range(5):
-        width = min(COLS, FLD - COLS * j)
-        part = tr[pl.ds(COLS * j, COLS), :].T[:, :width].reshape(NX, NY, width)
-        res[:, :, pl.ds(COLS * j, width)] = part
-    store = pltpu.make_async_copy(res, out, sem)
-    store.start()
-    store.wait()
+    drop = None
+    for i in range(RUN):
+        at = pl.ds(i, RUNS, stride=RUN)
+        drop = rain[at, :] if i == 0 else rain[at, :] + fac[4, at, :] * drop
+        rain[at, :] = drop
+    end = None
+    for r in range(RUNS):
+        part = rain[pl.ds(RUN * r, RUN), :]
+        if r:
+            part = part + fac[8, pl.ds(RUN * r, RUN), :] * end
+        tr[pl.ds(2 * LEV + RUN * r, RUN), :] = part
+        end = part[RUN - 1 :]
+    for j in (0, 1):
+        emit(j)
+    low = pl.ds(0, 2 * COLS)
+    stores.append(pltpu.make_async_copy(res.at[:, :, low], out.at[:, :, low], sem.at[1]))
+    stores[1].start()
+    for store in stores:
+        store.wait()
 
 
 def solution(mesh):
@@ -401,7 +461,7 @@
     def local(state, hyper, pmass, imass, slots, vdiff, frate, cfrac):
         fields, factors = pl.pallas_call(
             functools.partial(body, n_gx, n_gy),
-            out_shape=(pltpu.VMEM((5 * COLS, COLS), F32), pltpu.VMEM((6, LEV, COLS), F32)),
+            out_shape=(pltpu.VMEM((5 * COLS, COLS), F32), pltpu.VMEM((9, LEV, COLS), F32)),
             in_specs=[anywhere] * 10,
             out_specs=(inside, inside),
             scratch_shapes=[
@@ -422,8 +482,8 @@
                 pltpu.VMEM((1, FLD), F32),
                 pltpu.VMEM((COLS, 5 * COLS), F32),
                 dma((10,)),
-                dma((2, 8)),
-                dma((2, 8)),
+                dma((2, 3)),
+                dma((2, 3)),
                 dma((2,)),
                 dma((2,)),
                 pltpu.SemaphoreType.REGULAR((2,)),
@@ -441,7 +501,7 @@
                 pltpu.VMEM((LEV, VARS, COLS), F32),
                 pltpu.VMEM((LEV, COLS), F32),
                 pltpu.VMEM((NX, NY, FLD), F32),
-                dma,
+                dma((2,)),
             ],
         )(*(pltpu.with_memory_space_constraint(x, pltpu.VMEM) for x in (fields, factors)))
 

time: 34.5 us -> 34.2 us (level)
  no operation moved by 1% of the time
where the time goes in v5:
time: 34.2 us; the launch traced here: 34.1 us
  Pallas kernels  34.1 us (100%)
    pallas_call x1, Pallas kernels, local(): pl.pallas_call(functools.partial(body, n_gx, n_gy), out_shape=(pltpu.VMEM...  32.9 us
    pallas_call x1, Pallas kernels, local(): pl.pallas_call(columns, out_shape=jax.ShapeDtypeStruct((NX, NY, FLD), F32...  1.12 us

profile of v5, /device:TPU:7, one launch (start us, length us, event | category | flops | bytes accessed | tf_op | source)
XLA Modules:
  0.0 34.1 jit_solution(13460854117221302679)
XLA Ops:
  0.0 32.9 %shard_map.100 = (f32[640,128]{1,0:T(8,128)S(1)}, f32[9,48,128]{2,1,0:T(8,128)S(1)}) custom-call(f32[4,32,528]{2,1,0:T(8,128)} %state.1, f32[528]{0:T(1024)} %hyper.1, f32[4,32]{1,0:T(4,128)} %pmass.1, f32[4,32]{1,0:T(4,128)} %imass.1, s32[4,32]{1,0:T(4,128)} %slots.1, f32[1,48,128]{2,1,0:T(8,128)} %vdiff.1, f32[1,48,128]{2,1,0:T(8,128)} %frate.1, ...), custom_call_target="tpu_custom_call" | custom-call | tf_op jit(solution)/shard_map/pallas_call | solution.py:462
  32.9 1.1 %shard_map.101 = f32[4,32,528]{2,1,0:T(8,128)} custom-call(f32[640,128]{1,0:T(8,128)S(1)} %get-tuple-element.7.tin, f32[9,48,128]{2,1,0:T(8,128)S(1)} %get-tuple-element.8.fac), custom_call_target="tpu_custom_call" | custom-call | tf_op jit(solution)/shard_map/pallas_call | solution.py:494

commit v6 on v5

--- a/solution.py
+++ b/solution.py
@@ -213,19 +213,25 @@
         ]
         return copies, whole
 
-    def assemble(r):
-        acc[pl.ds(0, NY), :] = tsum[r, pl.ds(0, NY)] + xin[r, 0]
-        acc[pl.ds(NY, COLS - 2 * NY), :] = tsum[r, pl.ds(NY, COLS - 2 * NY)]
-        acc[pl.ds(COLS - NY, NY), :] = tsum[r, pl.ds(COLS - NY, NY)] + xin[r, 1]
+    def own_part(r):
+        acc[...] = inv_col * tsum[r]
+
+    def assemble(r, whole):
+        whole[0].wait_recv()
+        for part, at in ((0, 0), (1, COLS - NY)):
+            scale = inv_col[at : at + NY]
+            acc[pl.ds(at, NY), :] = acc[pl.ds(at, NY), :] + scale * xin[r, part]
+        whole[1].wait_recv()
+        whole[2].wait_recv()
         corner = {0: (0, 1), 3: (2, 3)}
         for x in range(NX):
             low, high = yin[r, 0, x], yin[r, 1, x]
             if x in corner:
                 low = low + cin[r, corner[x][0]]
                 high = high + cin[r, corner[x][1]]
-            acc[pl.ds(NY * x, 1), :] = acc[pl.ds(NY * x, 1), :] + low
-            acc[pl.ds(NY * x + NY - 1, 1), :] = acc[pl.ds(NY * x + NY - 1, 1), :] + high
-        return inv_col * acc[...]
+            for at, value in ((NY * x, low), (NY * x + NY - 1, high)):
+                acc[pl.ds(at, 1), :] = acc[pl.ds(at, 1), :] + inv_col[at : at + 1] * value
+        return acc[...]
 
     (first, first_all), (second, second_all) = halo(0), halo(1)
 
@@ -304,9 +310,9 @@
         weigh(0, v[...].reshape(COLS, FLD), first)
 
     def pass_again():
-        for copy in first_all:
-            copy.wait_recv()
-        weigh(1, assemble(0), second)
+        own_part(0)
+        weigh(1, assemble(0, first_all), second)
+        own_part(1)
 
     early = lax.rem(my, Z) < 2
 
@@ -373,9 +379,7 @@
             fac[target, at, :] = product
 
     loads[9].wait()
-    for copy in second_all:
-        copy.wait_recv()
-    dyn[:, pl.ds(0, FLD)] = v[...].reshape(COLS, FLD) - hyp[...] * assemble(1)
+    dyn[:, pl.ds(0, FLD)] = v[...].reshape(COLS, FLD) - hyp[...] * assemble(1, second_all)
     for j in range(5):
         tr[pl.ds(COLS * j, COLS), :] = dyn[:, pl.ds(COLS * j, COLS)].T
     slot_all.wait_send()

time: 34.2 us -> 34.2 us (level)
  no operation moved by 1% of the time
where the time goes in v6:
time: 34.2 us; the launch traced here: 34 us
  Pallas kernels  34 us (99%)
    pallas_call x1, Pallas kernels, local(): pl.pallas_call(functools.partial(body, n_gx, n_gy), out_shape=(pltpu.VMEM...  32.9 us
    pallas_call x1, Pallas kernels, local(): pl.pallas_call(columns, out_shape=jax.ShapeDtypeStruct((NX, NY, FLD), F32...  1.12 us

profile of v6, /device:TPU:7, one launch (start us, length us, event | category | flops | bytes accessed | tf_op | source)
XLA Modules:
  0.0 34.0 jit_solution(11653086029453570216)
XLA Ops:
  0.0 32.9 %shard_map.100 = (f32[640,128]{1,0:T(8,128)S(1)}, f32[9,48,128]{2,1,0:T(8,128)S(1)}) custom-call(f32[4,32,528]{2,1,0:T(8,128)} %state.1, f32[528]{0:T(1024)} %hyper.1, f32[4,32]{1,0:T(4,128)} %pmass.1, f32[4,32]{1,0:T(4,128)} %imass.1, s32[4,32]{1,0:T(4,128)} %slots.1, f32[1,48,128]{2,1,0:T(8,128)} %vdiff.1, f32[1,48,128]{2,1,0:T(8,128)} %frate.1, ...), custom_call_target="tpu_custom_call" | custom-call | tf_op jit(solution)/shard_map/pallas_call | solution.py:466
  32.9 1.1 %shard_map.101 = f32[4,32,528]{2,1,0:T(8,128)} custom-call(f32[640,128]{1,0:T(8,128)S(1)} %get-tuple-element.7.tin, f32[9,48,128]{2,1,0:T(8,128)S(1)} %get-tuple-element.8.fac), custom_call_target="tpu_custom_call" | custom-call | tf_op jit(solution)/shard_map/pallas_call | solution.py:498
